TPU v7x, 256 devices: a whole 4x4x8 slice. The times are simulated.
256 devices in a mesh: space: 32 (over y_hi, z, core), coil: 8 (over y_lo, x).
Axes of the slice: x: 4, y: 4 (y_hi: 2, y_lo: 2; y = y_hi * 2 + y_lo), z: 8, core: 2. Of those that a mesh axis runs over, the one named last changes fastest.
Arguments:
- spatial_coef: bfloat16 [16, 128, 128, 2, 128], P('coil', 'space'), may hold values from -6 to 6
- temporal_basis: bfloat16 [2, 16, 4], replicated, may hold values from -1.5 to 1.5
- coil_maps: bfloat16 [32, 128, 128, 2, 128], P('coil', 'space'), may hold values from -6 to 6
- field_steps: int32 [128, 128, 128], P('space'), may hold values from 0 to 255
- kspace_data: bfloat16 [32, 4, 128, 128, 2, 128], P('coil', None, None, 'space'), may hold values from -6 to 6
- sample_mask: int32 [4, 128, 128], P(None, 'space'), may hold values 0 or 1
Outputs:
- gradient: float32 [16, 128, 128, 2, 128], P('coil', 'space')
Inputs may be any that keep to these rules, and one draw needn't show every extreme that they name: `sample_mask`: 1 where a phase-encoding line is sampled at that point, else 0.
All inputs are finite; a program needn't handle non-finite values. No bound on the sum of `sample_mask` on one device may be relied on, other than what follows from the above.
Results may differ from a plain program's by a relative error of at most 0.014.
Values may be sent and summed in bfloat16 or wider, within the bound.
A program may use at most 64 MiB of HBM per device.

v0:
```python
import math

import jax
import jax.numpy as jnp
from jax import lax
from jax.sharding import PartitionSpec as P

STEPS_CYCLE = 256


def dft_table(length, sign):
    index = jnp.arange(length, dtype=jnp.int32)
    steps = index[:, None] * index[None, :] % length
    angle = steps.astype(jnp.float32) * (2.0 * math.pi / length)
    scale = 1.0 / math.sqrt(length)
    cosine = jnp.cos(angle) * scale
    sine = jnp.sin(angle) * (sign * scale)
    upper = jnp.stack([cosine, sine], axis=1)
    lower = jnp.stack([-sine, cosine], axis=1)
    return jnp.stack([upper, lower], axis=0).astype(jnp.bfloat16)


def forward_mix(basis):
    real_part = basis[0]
    imaginary = basis[1]
    return jnp.stack(
        [jnp.stack([real_part, imaginary], -1), jnp.stack([-imaginary, real_part], -1)], 1
    )


def adjoint_mix(basis):
    real_part = basis[0].T
    imaginary = basis[1].T
    return jnp.stack(
        [jnp.stack([real_part, -imaginary], -1), jnp.stack([imaginary, real_part], -1)], 1
    )


def phase_parts(field_steps, points):
    counter = jnp.arange(1, points + 1, dtype=jnp.int32)
    steps = field_steps[None] * counter[:, None, None, None] % STEPS_CYCLE
    angle = steps.astype(jnp.float32) * (2.0 * math.pi / STEPS_CYCLE)
    return (jnp.cos(angle), jnp.sin(angle))


def transform(volume, table, form):
    return jnp.einsum(form, volume, table, preferred_element_type=jnp.float32)


def shards(spatial_coef, temporal_basis, coil_maps, field_steps, kspace_data, sample_mask):
    points = temporal_basis.shape[2]
    section = temporal_basis
    image = jnp.einsum(
        "lxypz,lptq->txyqz",
        lax.all_gather(spatial_coef, "coil", axis=0, tiled=True),
        forward_mix(section),
        preferred_element_type=jnp.float32,
    )
    cosine, sine = phase_parts(field_steps, points)
    image_real = image[:, :, :, 0]
    image_imaginary = image[:, :, :, 1]
    turned_real = cosine * image_real - sine * image_imaginary
    turned_imaginary = sine * image_real + cosine * image_imaginary
    map_real = coil_maps[:, :, :, 0].astype(jnp.float32)[:, None]
    map_imaginary = coil_maps[:, :, :, 1].astype(jnp.float32)[:, None]
    coil_real = map_real * turned_real - map_imaginary * turned_imaginary
    coil_imaginary = map_real * turned_imaginary + map_imaginary * turned_real
    coil_image = jnp.stack([coil_real, coil_imaginary], axis=4).astype(jnp.bfloat16)
    depth_count = coil_image.shape[5]
    row_count = coil_image.shape[3]
    depth_pass = transform(coil_image, dft_table(depth_count, -1.0), "ctxypz,pzqk->ctxyqk").astype(
        jnp.bfloat16
    )
    row_pass = transform(depth_pass, dft_table(row_count, -1.0), "ctxypz,pyqk->ctxkqz").astype(
        jnp.bfloat16
    )
    slabs = lax.all_to_all(row_pass, "space", split_axis=3, concat_axis=2, tiled=True)
    first_count = slabs.shape[2]
    kspace = transform(slabs, dft_table(first_count, -1.0), "ctxypz,pxqk->ctkyqz")
    mask_float = sample_mask.astype(jnp.float32)[None, :, None, :, None, :]
    residual = (mask_float * (kspace - kspace_data.astype(jnp.float32))).astype(jnp.bfloat16)
    back_first = transform(residual, dft_table(first_count, 1.0), "ctxypz,pxqk->ctkyqz").astype(
        jnp.bfloat16
    )
    returned = lax.all_to_all(back_first, "space", split_axis=2, concat_axis=3, tiled=True)
    back_rows = transform(returned, dft_table(row_count, 1.0), "ctxypz,pyqk->ctxkqz").astype(
        jnp.bfloat16
    )
    back_image = transform(back_rows, dft_table(depth_count, 1.0), "ctxypz,pzqk->ctxyqk")
    back_real = back_image[:, :, :, :, 0]
    back_imaginary = back_image[:, :, :, :, 1]
    sum_real = jnp.sum(map_real * back_real + map_imaginary * back_imaginary, axis=0)
    sum_imaginary = jnp.sum(map_real * back_imaginary - map_imaginary * back_real, axis=0)
    combined_real = cosine * sum_real + sine * sum_imaginary
    combined_imaginary = cosine * sum_imaginary - sine * sum_real
    combined = jnp.stack([combined_real, combined_imaginary], axis=3)
    section = temporal_basis.astype(jnp.float32)
    return lax.psum_scatter(
        jnp.einsum(
            "txypz,tplq->lxyqz", combined, adjoint_mix(section), precision=lax.Precision.HIGHEST
        ).astype(jnp.bfloat16),
        "coil",
        scatter_dimension=0,
        tiled=True,
    ).astype(jnp.float32)


def solution(mesh):
    in_specs = (
        P("coil", "space", None, None, None),
        P(),
        P("coil", "space", None, None, None),
        P("space", None, None),
        P("coil", None, None, "space", None, None),
        P(None, "space", None),
    )
    out_specs = P("coil", "space", None, None, None)
    return jax.shard_map(shards, mesh=mesh, in_specs=in_specs, out_specs=out_specs, check_vma=False)
```

profile of v0, /device:TPU:16, one launch (start us, length us, event | category | flops | bytes accessed | tf_op | source)
XLA Modules:
  0.0 417.0 jit_solution(10272380356210166558)
XLA Ops:
  6.5 1.9 copy.65
  8.5 0.0 all-gather.2.cloned.1.call-update
  8.5 0.7 fusion.72
  9.2 0.7 slice_bitcast_fusion.6
  9.9 0.3 multiply_convert_fusion.2
  10.2 0.3 negate_convert_fusion
  10.5 0.3 multiply_convert_fusion
  10.8 3.6 slice_convert_fusion.1
  14.4 52.4 %all-gather.2.cloned.1.call-done = bf16[16,4,128,2,128]{4,2,3,1,0:T(8,128)(2,1)} async-done(((bf16[2,4,128,2,128]{4,2,3,1,0:T(8,128)(2,1)}), bf16[16,4,128,2,128]{4,2,3,1,0:T(8,128)(2,1)}) %all-gather.2.cloned.1.call-update) | async-done | bytes 4194320 | tf_op jit(solution)/shard_map/all_gather | solution.py:55
  66.8 4.9 %fusion.31 = f32[4,2,4,128,128]{4,0,3,2,1:T(4,128)S(1)} fusion(bf16[16,4,128,2,128]{4,2,3,1,0:T(8,128)(2,1)} %all-gather.2.cloned.1.call-done, bf16[16,1,4,2]{0,2,1,3:T(4,128)(2,1)S(1)} %get-tuple-element.26, bf16[16,1,4,2]{0,2,1,3:T(4,128)(2,1)S(1)} %get-tuple-element.25), kind=kOutput, calls=%fused_computation.43 | convolution fusion | flops 33555456 | bytes 6291968 | tf_op jit(solution)/shard_map/lxypz,lptq->txyqz/dot_general | solution.py:53
  71.7 0.3 copy.134
  71.9 4.6 %multiply_subtract_fusion = (f32[4,4,128,128]{3,2,1,0:T(8,128)S(1)}, f32[4,4,128,128]{3,2,1,0:T(8,128)S(1)}) fusion(f32[4,4,128,2,128]{4,2,1,0,3:T(8,128)S(1)} %bitcast.244, s32[4]{0:T(128)S(1)} %iota_add_fusion, s32[4,128,128]{2,1,0:T(8,128)S(1)} %copy-done.1), kind=kLoop, calls=%fused_computation.64 | loop fusion | flops 5242880 | bytes 4456464 | tf_op jit(solution)/shard_map/sub | solution.py:62
  76.6 3.1 subtract_convert_fusion
  79.7 6.7 %fusion.5 = bf16[4,4,4,128,2,128]{5,3,2,1,0,4:T(8,128)(2,1)} fusion(bf16[4,4,4,128,1,128]{5,3,4,2,1,0:T(8,128)(2,1)} %get-tuple-element.8, bf16[4,4,4,128,1,128]{5,3,4,2,1,0:T(8,128)(2,1)} %get-tuple-element.7, bf16[1,128,2,128]{3,1,0,2:T(8,128)(2,1)S(1)} %get-tuple-element.16, bf16[1,128,2,128]{3,1,0,2:T(8,128)(2,1)S(1)} %get-tuple-element.17), kind=kOutput, calls=%fused_computation.10 | convolution fusion | flops 2160590848 | bytes 8519680 | tf_op jit(solution)/shard_map/ctxypz,pyqk->ctxkqz/dot_general | solution.py:47
  86.4 7.4 %copy.69 = bf16[4,4,4,128,2,128]{5,2,1,0,4,3:T(4,128)(2,1)} copy(bf16[4,4,4,128,2,128]{5,3,2,1,0,4:T(8,128)(2,1)} %fusion.5) | data formatting | bytes 8388608 | tf_op jit(solution)/shard_map/convert_element_type | solution.py:74
  93.8 10.3 %all-to-all-start = ((bf16[4,4,4,128,2,128]{5,2,1,0,4,3:T(4,128)(2,1)}), bf16[4,4,4,128,2,128]{5,2,1,0,4,3:T(4,128)(2,1)}, u32[]{:S(2)}, u32[]{:S(2)}) async-start(bf16[4,4,4,128,2,128]{5,2,1,0,4,3:T(4,128)(2,1)} %copy.69), calls=%async_computation | async-start | bytes 8388608 | tf_op jit(solution)/shard_map/all_to_all | solution.py:77
  104.2 94.0 %all-to-all-done = bf16[4,4,4,128,2,128]{5,2,1,0,4,3:T(4,128)(2,1)} async-done(((bf16[4,4,4,128,2,128]{5,2,1,0,4,3:T(4,128)(2,1)}), bf16[4,4,4,128,2,128]{5,2,1,0,4,3:T(4,128)(2,1)}, u32[]{:S(2)}, u32[]{:S(2)}) %all-to-all-start) | async-done | bytes 4194336 | tf_op jit(solution)/shard_map/all_to_all | solution.py:77
  198.2 4.7 %copy.70 = bf16[4,4,4,32,4,2,128]{6,2,3,5,4,1,0:T(4,128)(2,1)S(1)} copy(bf16[4,4,4,32,4,2,128]{6,2,1,0,5,4,3:T(4,128)(2,1)} %bitcast.51) | data formatting | bytes 8388608 | tf_op jit(solution)/shard_map/all_to_all | solution.py:77
  202.9 1.4 fusion.1
  204.3 1.3 fusion.6
  205.6 5.2 %copy.75 = bf16[4,4,128,4,2,128]{5,3,1,0,4,2:T(4,128)(2,1)} copy(bf16[4,4,128,4,2,128]{5,2,3,1,0,4:T(8,128)(2,1)S(1)} %fusion.6) | data formatting | bytes 8388608 | tf_op jit(solution)/shard_map/convert_element_type | solution.py:82
  210.8 9.5 %all-to-all-start.1 = ((bf16[4,4,128,4,2,128]{5,3,1,0,4,2:T(4,128)(2,1)}), bf16[4,4,128,4,2,128]{5,3,1,0,4,2:T(4,128)(2,1)}, u32[]{:S(2)}, u32[]{:S(2)}) async-start(bf16[4,4,128,4,2,128]{5,3,1,0,4,2:T(4,128)(2,1)} %copy.75), calls=%async_computation.1 | async-start | bytes 8388608 | tf_op jit(solution)/shard_map/all_to_all | solution.py:85
  220.3 0.0 reduce-scatter.2.cloned.1.call-start
  220.4 93.9 %all-to-all-done.1 = bf16[4,4,128,4,2,128]{5,3,1,0,4,2:T(4,128)(2,1)} async-done(((bf16[4,4,128,4,2,128]{5,3,1,0,4,2:T(4,128)(2,1)}), bf16[4,4,128,4,2,128]{5,3,1,0,4,2:T(4,128)(2,1)}, u32[]{:S(2)}, u32[]{:S(2)}) %all-to-all-start.1) | async-done | bytes 4194336 | tf_op jit(solution)/shard_map/all_to_all | solution.py:85
  314.4 6.5 %copy.76 = bf16[4,4,32,4,4,2,128]{6,4,2,5,3,1,0:T(4,128)(2,1)} copy(bf16[4,4,32,4,4,2,128]{6,4,1,0,5,3,2:T(4,128)(2,1)} %bitcast.62) | data formatting | bytes 8388608 | tf_op jit(solution)/shard_map/all_to_all | solution.py:85
  320.9 7.8 %fusion.20 = f32[4,4,4,128,2,128]{5,3,4,2,1,0:T(8,128)} fusion(bf16[4,4,4,128,2,128,1]{5,3,6,4,2,1,0:T(8,128)(2,1)} %bitcast.238, bf16[1,128,2,128]{3,1,2,0:T(8,128)(2,1)S(1)} %get-tuple-element.18, bf16[1,128,2,128]{3,1,2,0:T(8,128)(2,1)S(1)} %get-tuple-element.15), kind=kOutput, calls=%fused_computation.31 | convolution fusion | flops 2150105088 | bytes 12713984 | tf_op jit(solution)/shard_map/ctxypz,pzqk->ctxyqk/dot_general | solution.py:47
  328.7 4.6 %add_reduce_fusion = (f32[4,4,128,128]{3,2,1,0:T(8,128)S(1)}, f32[4,4,128,128]{3,2,1,0:T(8,128)S(1)}) fusion(f32[4,4,4,128,2,128]{5,3,4,2,1,0:T(8,128)} %fusion.20, f32[4,4,128,128]{3,2,1,0:T(8,128)S(1)} %bitcast.243, f32[4,4,128,128]{3,2,1,0:T(8,128)S(1)} %bitcast.241), kind=kLoop, calls=%fused_computation.28 | loop fusion | flops 7864320 | bytes 12582912 | tf_op jit(solution)/shard_map/reduce_sum | solution.py:92
  333.3 9.6 %fusion.40 = (f32[4,4,128,1,128]{4,0,3,2,1:T(4,128)S(1)}, f32[4,4,128,1,128]{4,0,3,2,1:T(4,128)S(1)}) fusion(f32[4,4,128,128]{3,2,1,0:T(8,128)S(1)} %get-tuple-element.6, f32[4,4,128,128]{3,2,1,0:T(8,128)S(1)} %get-tuple-element.5, s32[4]{0:T(128)S(1)} %iota_add_fusion, s32[4,128,128]{2,1,0:T(8,128)S(1)} %copy-done.1), kind=kLoop, calls=%fused_computation.58 | loop fusion | flops 5242880 | bytes 4456464 | tf_op jit(solution)/shard_map/add | solution.py:94
  342.9 7.8 %fusion.7 = bf16[16,4,128,2,128]{4,0,2,1,3:T(8,128)(2,1)S(1)} fusion(f32[4,4,128,1,128]{4,0,3,2,1:T(4,128)S(1)} %get-tuple-element.10, f32[4,4,128,1,128]{4,0,3,2,1:T(4,128)S(1)} %get-tuple-element.9, f32[4,1,16,2]{2,0,1,3:T(4,128)S(1)} %get-tuple-element.22, f32[4,1,16,2]{2,0,1,3:T(4,128)S(1)} %get-tuple-element.21), kind=kOutput, calls=%fused_computation.12 | convolution fusion | flops 203948288 | bytes 6292480 | tf_op jit(solution)/shard_map/txypz,tplq->lxyqz/dot_general | solution.py:99
  350.7 3.1 copy.82
  353.8 53.8 %reduce-scatter.2.cloned.1.call-done = bf16[2,4,128,2,128]{4,2,3,1,0:T(8,128)(2,1)} async-done(((bf16[16,4,128,2,128]{4,2,3,1,0:T(8,128)(2,1)}), bf16[2,4,128,2,128]{4,2,3,1,0:T(8,128)(2,1)}) %reduce-scatter.2.cloned.1.call-update) | async-done | bytes 524304 | tf_op jit(solution)/shard_map/reduce_scatter | solution.py:98
  407.6 2.6 copy.83
  (18 shorter events, 0.1 us)
Async XLA Ops:
  6.5 60.3 %all-gather.2.cloned.1.call-start = ((), (), s32[]{:S(2)}) async-start(), calls=%async_computation.3 | async-start | bytes 4718592 | tf_op jit(solution)/shard_map/all_gather | solution.py:55
  66.8 5.1 %copy-start.1 = (s32[4,128,128]{2,1,0:T(8,128)S(1)}, s32[4,128,128]{2,1,0:T(8,128)}, u32[]{:S(2)}) copy-start(s32[4,128,128]{2,1,0:T(8,128)} %param.9) | copy-start | bytes 786436
  93.8 10.3 %copy-start.3 = (s32[4,4,128]{2,1,0:T(4,128)S(1)}, s32[4,4,128]{2,1,0:T(4,128)}, u32[]{:S(2)}) copy-start(s32[4,4,128]{2,1,0:T(4,128)} %param.11) | copy-start | bytes 24580
  93.8 104.4 %all-to-all-start = ((bf16[4,4,4,128,2,128]{5,2,1,0,4,3:T(4,128)(2,1)}), bf16[4,4,4,128,2,128]{5,2,1,0,4,3:T(4,128)(2,1)}, u32[]{:S(2)}, u32[]{:S(2)}) async-start(bf16[4,4,4,128,2,128]{5,2,1,0,4,3:T(4,128)(2,1)} %copy.69), calls=%async_computation | async-start | bytes 8388608 | tf_op jit(solution)/shard_map/all_to_all | solution.py:77
  198.2 4.7 %copy-start = (bf16[4,4,128,4,2,128]{5,4,3,2,1,0:T(2,128)(2,1)S(1)}, bf16[4,4,128,4,2,128]{5,4,3,2,1,0:T(2,128)(2,1)}, u32[]{:S(2)}) copy-start(bf16[4,4,128,4,2,128]{5,4,3,2,1,0:T(2,128)(2,1)} %param.10) | copy-start | bytes 12582916
  210.8 9.6 %copy-start.2 = (bf16[2,16,4]{1,2,0:T(4,128)(2,1)S(1)}, bf16[2,16,4]{1,2,0:T(4,128)(2,1)}, u32[]{:S(2)}) copy-start(bf16[2,16,4]{1,2,0:T(4,128)(2,1)} %param.7) | copy-start | bytes 772
  210.8 103.6 %all-to-all-start.1 = ((bf16[4,4,128,4,2,128]{5,3,1,0,4,2:T(4,128)(2,1)}), bf16[4,4,128,4,2,128]{5,3,1,0,4,2:T(4,128)(2,1)}, u32[]{:S(2)}, u32[]{:S(2)}) async-start(bf16[4,4,128,4,2,128]{5,3,1,0,4,2:T(4,128)(2,1)} %copy.75), calls=%async_computation.1 | async-start | bytes 8388608 | tf_op jit(solution)/shard_map/all_to_all | solution.py:85
  220.3 187.3 %reduce-scatter.2.cloned.1.call-start = ((), (), s32[]{:S(2)}) async-start(), calls=%async_computation.4 | async-start | bytes 4718592 | tf_op jit(solution)/shard_map/reduce_scatter | solution.py:98
Sparse Core Ops, SparseCore 0:
  9.1 57.6 all-gather.1
  353.9 53.6 reduce-scatter.1
where the time goes:
time: 419 us; the launch traced here: 417 us
  waiting for transfers between devices  294 us (70%)
  local copies, waits for them, and re-layouts  32.4 us (8%)
  matrix products  29.8 us (7%)
  other arithmetic  27.2 us (6%)
  starting transfers between devices  19.9 us (5%)
  between operations  13.6 us (3%)
    all_to_all x1, waiting for transfers between devices, shards(): lax.all_to_all(row_pass, 'space', split_axis=3, concat_axis=2, tiled=True)  94 us
    all_to_all x1, waiting for transfers between devices, shards(): lax.all_to_all(back_first, 'space', split_axis=2, concat_axis=3, tiled=True)  93.9 us
    reduce_scatter x1, waiting for transfers between devices, shards(): lax.psum_scatter(jnp.einsum('txypz,tplq->lxyqz', combined, adjoint_mix(se...  53.8 us
    all_gather x1, waiting for transfers between devices, shards(): lax.all_gather(spatial_coef, 'coil', axis=0, tiled=True)  52.4 us
    dot_general x4, matrix products, transform(): return jnp.einsum(form, volume, table, preferred_element_type=jnp.float32)  17.2 us
    all_to_all x1, starting transfers between devices, shards(): lax.all_to_all(row_pass, 'space', split_axis=3, concat_axis=2, tiled=True)  10.3 us
    add x1, other arithmetic, shards(): combined_real = cosine * sum_real + sine * sum_imaginary  9.64 us
    all_to_all x1, starting transfers between devices, shards(): lax.all_to_all(back_first, 'space', split_axis=2, concat_axis=3, tiled=True)  9.54 us
  transfers between devices with their start and end apart: 4, of which 4 were waited for; matrix products, arithmetic and copies ran while one was open for 1% of the time, Pallas kernels for 0%

commit v1 on v0

--- a/solution.py
+++ b/solution.py
@@ -50,6 +50,12 @@
 def shards(spatial_coef, temporal_basis, coil_maps, field_steps, kspace_data, sample_mask):
     points = temporal_basis.shape[2]
     section = temporal_basis
+    data_first = transform(
+        kspace_data, dft_table(kspace_data.shape[2], 1.0), "ctxypz,pxqk->ctkyqz"
+    ).astype(jnp.bfloat16)
+    measured = lax.all_to_all(data_first, "space", split_axis=2, concat_axis=3, tiled=True)
+    mask_all = lax.all_gather(sample_mask.astype(jnp.bfloat16), "space", axis=1, tiled=True)
+    mask_all = mask_all.astype(jnp.float32)[None, :, None, :, None, :]
     image = jnp.einsum(
         "lxypz,lptq->txyqz",
         lax.all_gather(spatial_coef, "coil", axis=0, tiled=True),
@@ -71,19 +77,9 @@
     depth_pass = transform(coil_image, dft_table(depth_count, -1.0), "ctxypz,pzqk->ctxyqk").astype(
         jnp.bfloat16
     )
-    row_pass = transform(depth_pass, dft_table(row_count, -1.0), "ctxypz,pyqk->ctxkqz").astype(
-        jnp.bfloat16
-    )
-    slabs = lax.all_to_all(row_pass, "space", split_axis=3, concat_axis=2, tiled=True)
-    first_count = slabs.shape[2]
-    kspace = transform(slabs, dft_table(first_count, -1.0), "ctxypz,pxqk->ctkyqz")
-    mask_float = sample_mask.astype(jnp.float32)[None, :, None, :, None, :]
-    residual = (mask_float * (kspace - kspace_data.astype(jnp.float32))).astype(jnp.bfloat16)
-    back_first = transform(residual, dft_table(first_count, 1.0), "ctxypz,pxqk->ctkyqz").astype(
-        jnp.bfloat16
-    )
-    returned = lax.all_to_all(back_first, "space", split_axis=2, concat_axis=3, tiled=True)
-    back_rows = transform(returned, dft_table(row_count, 1.0), "ctxypz,pyqk->ctxkqz").astype(
+    row_pass = transform(depth_pass, dft_table(row_count, -1.0), "ctxypz,pyqk->ctxkqz")
+    residual = (mask_all * (row_pass - measured.astype(jnp.float32))).astype(jnp.bfloat16)
+    back_rows = transform(residual, dft_table(row_count, 1.0), "ctxypz,pyqk->ctxkqz").astype(
         jnp.bfloat16
     )
     back_image = transform(back_rows, dft_table(depth_count, 1.0), "ctxypz,pzqk->ctxyqk")

time: 419 us -> 292 us (0.70)
  waiting for transfers between devices: 294 us -> 50.5 us
  blocking collectives: 0 us -> 132 us
  local copies, waits for them, and re-layouts: 32.4 us -> 20.6 us
  starting transfers between devices: 19.9 us -> 11.8 us
  matrix products: 29.8 us -> 35.8 us
    all_to_all x2 -> x1, waiting for transfers between devices: 188 us -> 0.01 us  [shards(): lax.all_to_all(data_first, 'space', split_axis=2, concat_axis=3, tiled=True)]
    all_gather x0 -> x1, blocking collectives: none -> 132 us  [shards(): lax.all_gather(sample_mask.astype(jnp.bfloat16), 'space', axis=1, tiled=T...]
    all_gather x1, waiting for transfers between devices: 52.4 us -> 0.02 us  [shards(): lax.all_gather(spatial_coef, 'coil', axis=0, tiled=True)]
    all_to_all x2 -> x0, local copies, waits for them, and re-layouts: 11.2 us -> none  [the longest x1 6.52 us: shards(): lax.all_to_all(back_first, 'space', split_axis=2, concat_axis=3, tiled=True)]
    all_to_all x2 -> x1, starting transfers between devices: 19.9 us -> 11.8 us  [shards(): lax.all_to_all(data_first, 'space', split_axis=2, concat_axis=3, tiled=True)]
    dot_general x4 -> x3, matrix products: 17.2 us -> 23 us  [transform(): return jnp.einsum(form, volume, table, preferred_element_type=jnp.float32)]
  transfers between devices with their start and end apart: 4 -> 3, of which waited for: 4 -> 1; matrix products, arithmetic and copies ran while one was open for 1% -> 12% of each run, Pallas kernels for 0% -> 0%
where the time goes in v1:
time: 292 us; the launch traced here: 290 us
  blocking collectives  132 us (45%)
  waiting for transfers between devices  50.5 us (17%)
  matrix products  35.8 us (12%)
  other arithmetic  26 us (9%)
  local copies, waits for them, and re-layouts  20.6 us (7%)
  between operations  13.6 us (5%)
  starting transfers between devices  11.8 us (4%)
    all_gather x1, blocking collectives, shards(): lax.all_gather(sample_mask.astype(jnp.bfloat16), 'space', axis=1, tiled=T...  132 us
    reduce_scatter x1, waiting for transfers between devices, shards(): lax.psum_scatter(jnp.einsum('txypz,tplq->lxyqz', combined, adjoint_mix(se...  50.4 us
    dot_general x3, matrix products, transform(): return jnp.einsum(form, volume, table, preferred_element_type=jnp.float32)  23 us
    all_to_all x1, starting transfers between devices, shards(): lax.all_to_all(data_first, 'space', split_axis=2, concat_axis=3, tiled=True)  11.8 us
    add x1, other arithmetic, shards(): combined_real = cosine * sum_real + sine * sum_imaginary  9.64 us
    dot_general x1, matrix products, shards(): jnp.einsum('txypz,tplq->lxyqz', combined, adjoint_mix(section), precision...  7.99 us
    convert_element_type x1, local copies, waits for them, and re-layouts, shards(): measured.astype(jnp.float32)  7.58 us
  transfers between devices with their start and end apart: 3, of which 1 were waited for; matrix products, arithmetic and copies ran while one was open for 12% of the time, Pallas kernels for 0%

profile of v1, /device:TPU:16, one launch (start us, length us, event | category | flops | bytes accessed | tf_op | source)
XLA Modules:
  0.0 290.4 jit_solution(16822251822179773445)
XLA Ops:
  6.5 1.9 copy.62
  8.5 0.0 all-gather.2.cloned.1.call-update
  8.5 0.3 negate_convert_fusion
  8.8 0.3 multiply_convert_fusion
  9.1 0.3 multiply_convert_fusion.2
  9.3 0.7 fusion.59
  10.0 3.5 %fusion.5 = bf16[4,4,128,4,2,128]{5,2,3,1,0,4:T(8,128)(2,1)S(1)} fusion(bf16[4,4,128,4,2,128]{5,4,3,2,1,0:T(2,128)(2,1)} %param.10, bf16[1,128,2,128]{3,1,2,0:T(8,128)(2,1)S(1)} %get-tuple-element.17, bf16[1,128,2,128]{3,1,2,0:T(8,128)(2,1)S(1)} %get-tuple-element.18), kind=kOutput, calls=%fused_computation.9 | convolution fusion | flops 1075904512 | bytes 8519680 | tf_op jit(solution)/shard_map/ctxypz,pxqk->ctkyqz/dot_general | solution.py:47
  13.5 5.2 %copy.68 = bf16[4,4,128,4,2,128]{5,3,1,0,4,2:T(4,128)(2,1)} copy(bf16[4,4,128,4,2,128]{5,2,3,1,0,4:T(8,128)(2,1)S(1)} %fusion.5) | data formatting | bytes 8388608 | tf_op jit(solution)/shard_map/convert_element_type | solution.py:55
  18.7 11.8 %all-to-all-start = ((bf16[4,4,128,4,2,128]{5,3,1,0,4,2:T(4,128)(2,1)}), bf16[4,4,128,4,2,128]{5,3,1,0,4,2:T(4,128)(2,1)}, u32[]{:S(2)}, u32[]{:S(2)}) async-start(bf16[4,4,128,4,2,128]{5,3,1,0,4,2:T(4,128)(2,1)} %copy.68), calls=%async_computation | async-start | bytes 8388608 | tf_op jit(solution)/shard_map/all_to_all | solution.py:56
  30.5 0.0 reduce-scatter.2.cloned.1.call-start
  30.6 0.0 copy-done.4
  30.6 0.0 copy-done.5
  30.6 132.1 %all_gather.6 = bf16[4,128,128]{2,0,1:T(4,128)(2,1)S(1)} all-gather(bf16[4,4,128]{2,0,1:T(4,128)(2,1)S(1)} %copy_convert_fusion.1), channel_id=1, replica_groups=mesh['space'=32,'coil'=8] {'space'}, dimensions={1}, use_global_device_ids=true | all-gather | bytes 135168 | tf_op jit(solution)/shard_map/all_gather | solution.py:57
  162.7 0.5 iota_add_fusion
  163.3 2.2 slice_convert_fusion.1
  165.5 0.0 all-gather.2.cloned.1.call-done
  165.5 0.0 copy-start.1
  165.6 4.9 %fusion.36 = f32[4,2,4,128,128]{4,0,3,2,1:T(4,128)S(1)} fusion(bf16[16,4,128,2,128]{4,2,3,1,0:T(8,128)(2,1)} %all-gather.2.cloned.1.call-done, bf16[16,1,4,2]{0,2,1,3:T(4,128)(2,1)S(1)} %get-tuple-element.26, bf16[16,1,4,2]{0,2,1,3:T(4,128)(2,1)S(1)} %get-tuple-element.25), kind=kOutput, calls=%fused_computation.43 | convolution fusion | flops 33555456 | bytes 6291968 | tf_op jit(solution)/shard_map/lxypz,lptq->txyqz/dot_general | solution.py:59
  170.4 0.3 copy.124
  170.7 4.6 %multiply_subtract_fusion = (f32[4,4,128,128]{3,2,1,0:T(8,128)S(1)}, f32[4,4,128,128]{3,2,1,0:T(8,128)S(1)}) fusion(f32[4,4,128,2,128]{4,2,1,0,3:T(8,128)S(1)} %bitcast.236, s32[4]{0:T(128)S(1)} %copy-done.6, s32[4,128,128]{2,1,0:T(8,128)S(1)} %copy-done.1), kind=kLoop, calls=%fused_computation.64 | loop fusion | flops 5242880 | bytes 4456464 | tf_op jit(solution)/shard_map/sub | solution.py:68
  175.4 3.1 %subtract_convert_fusion = (bf16[4,4,4,128,1,128]{5,3,4,2,1,0:T(8,128)(2,1)}, bf16[4,4,4,128,1,128]{5,3,4,2,1,0:T(8,128)(2,1)}) fusion(f32[4,4,128,128]{3,2,1,0:T(8,128)S(1)} %get-tuple-element.12, f32[4,4,128,128]{3,2,1,0:T(8,128)S(1)} %bitcast.234, f32[4,4,128,128]{3,2,1,0:T(8,128)S(1)} %get-tuple-element.11, f32[4,4,128,128]{3,2,1,0:T(8,128)S(1)} %bitcast.232), kind=kLoop, calls=%fused_computation.30 | loop fusion | flops 8388608 | bytes 8388608 | tf_op jit(solution)/shard_map/convert.5
  178.4 8.0 %fusion.3 = f32[2,128,4,4,4,128,1]{5,1,6,0,4,3,2:T(8,128)} fusion(bf16[4,4,4,128,1,128]{5,3,4,2,1,0:T(8,128)(2,1)} %get-tuple-element.8, bf16[4,4,4,128,1,128]{5,3,4,2,1,0:T(8,128)(2,1)} %get-tuple-element.7, bf16[1,128,2,128]{3,1,0,2:T(8,128)(2,1)S(1)} %copy-done.3, bf16[1,128,2,128]{3,1,0,2:T(8,128)(2,1)S(1)} %copy-done.2), kind=kOutput, calls=%fused_computation.8 | convolution fusion | flops 2158493696 | bytes 12713984 | tf_op jit(solution)/shard_map/ctxypz,pyqk->ctxkqz/dot_general | solution.py:47
  186.4 0.0 all-to-all-done
  186.4 7.6 %copy.69 = f32[4,4,32,4,4,2,128]{6,4,2,5,3,1,0:T(4,128)} copy(bf16[4,4,32,4,4,2,128]{6,4,1,0,5,3,2:T(4,128)(2,1)} %bitcast.88) | data formatting | bytes 12582912 | tf_op jit(solution)/shard_map/convert_element_type | solution.py:81
  194.0 11.5 %fusion.27 = f32[4,4,4,128,2,128]{5,3,4,2,1,0:T(8,128)} fusion(f32[4,4,4,128,2,128]{5,3,4,2,1,0:T(8,128)} %bitcast.231, f32[2,128,4,4,4,128,1]{5,1,6,0,4,3,2:T(8,128)} %fusion.3, f32[4,128,128]{2,1,0:T(8,128)S(1)} %copy_convert_fusion, bf16[1,128,2,128]{3,1,2,0:T(8,128)(2,1)S(1)} %get-tuple-element.17, bf16[1,128,2,128]{3,1,2,0:T(8,128)(2,1)S(1)} %get-tuple-element.18), kind=kOutput, calls=%fused_computation.32 | convolution fusion | flops 2156396544 | bytes 25559040 | tf_op jit(solution)/shard_map/ctxypz,pzqk->ctxyqk/dot_general | solution.py:47
  205.5 4.3 %add_reduce_fusion = (f32[4,4,128,128]{3,2,1,0:T(8,128)S(1)}, f32[4,4,128,128]{3,2,1,0:T(8,128)S(1)}) fusion(f32[4,4,4,128,2,128]{5,3,4,2,1,0:T(8,128)} %fusion.27, f32[4,4,128,128]{3,2,1,0:T(8,128)S(1)} %bitcast.235, f32[4,4,128,128]{3,2,1,0:T(8,128)S(1)} %bitcast.233), kind=kLoop, calls=%fused_computation.28 | loop fusion | flops 7864320 | bytes 12582912 | tf_op jit(solution)/shard_map/reduce_sum | solution.py:88
  209.8 9.6 %fusion.45 = (f32[4,4,128,1,128]{4,0,3,2,1:T(4,128)S(1)}, f32[4,4,128,1,128]{4,0,3,2,1:T(4,128)S(1)}) fusion(f32[4,4,128,128]{3,2,1,0:T(8,128)S(1)} %get-tuple-element.6, f32[4,4,128,128]{3,2,1,0:T(8,128)S(1)} %get-tuple-element.5, s32[4]{0:T(128)S(1)} %copy-done.6, s32[4,128,128]{2,1,0:T(8,128)S(1)} %copy-done.1), kind=kLoop, calls=%fused_computation.58 | loop fusion | flops 5242880 | bytes 4456464 | tf_op jit(solution)/shard_map/add | solution.py:90
  219.5 8.0 %fusion.6 = bf16[16,4,128,2,128]{4,0,2,1,3:T(8,128)(2,1)S(1)} fusion(f32[4,4,128,1,128]{4,0,3,2,1:T(4,128)S(1)} %get-tuple-element.10, f32[4,4,128,1,128]{4,0,3,2,1:T(4,128)S(1)} %get-tuple-element.9, f32[4,1,16,2]{2,0,1,3:T(4,128)S(1)} %get-tuple-element.22, f32[4,1,16,2]{2,0,1,3:T(4,128)S(1)} %get-tuple-element.21), kind=kOutput, calls=%fused_computation.10 | convolution fusion | flops 203948288 | bytes 6292480 | tf_op jit(solution)/shard_map/txypz,tplq->lxyqz/dot_general | solution.py:95
  227.5 3.1 %copy.75 = bf16[16,4,128,2,128]{4,2,3,1,0:T(8,128)(2,1)} copy(bf16[16,4,128,2,128]{4,0,2,1,3:T(8,128)(2,1)S(1)} %fusion.6) | data formatting | bytes 8388608 | tf_op jit(solution)/shard_map/convert_element_type | solution.py:97
  230.6 0.0 reduce-scatter.2.cloned.1.call-update
  230.6 50.4 %reduce-scatter.2.cloned.1.call-done = bf16[2,4,128,2,128]{4,2,3,1,0:T(8,128)(2,1)} async-done(((bf16[16,4,128,2,128]{4,2,3,1,0:T(8,128)(2,1)}), bf16[2,4,128,2,128]{4,2,3,1,0:T(8,128)(2,1)}) %reduce-scatter.2.cloned.1.call-update) | async-done | bytes 524304 | tf_op jit(solution)/shard_map/reduce_scatter | solution.py:94
  281.0 2.6 copy.76
  (21 shorter events, 0.1 us)
Async XLA Ops:
  6.5 159.0 %all-gather.2.cloned.1.call-start = ((), (), s32[]{:S(2)}) async-start(), calls=%async_computation.2 | async-start | bytes 4718592 | tf_op jit(solution)/shard_map/all_gather | solution.py:61
  18.7 11.8 %copy-start.4 = (bf16[2,16,4]{1,2,0:T(4,128)(2,1)S(1)}, bf16[2,16,4]{1,2,0:T(4,128)(2,1)}, u32[]{:S(2)}) copy-start(bf16[2,16,4]{1,2,0:T(4,128)(2,1)} %param.7) | copy-start | bytes 772
  18.7 11.9 %copy-start.5 = (s32[4,4,128]{2,1,0:T(4,128)S(1)}, s32[4,4,128]{2,1,0:T(4,128)}, u32[]{:S(2)}) copy-start(s32[4,4,128]{2,1,0:T(4,128)} %param.11) | copy-start | bytes 24580
  18.7 144.6 %copy-start = (bf16[4,4,128,2,128]{4,3,2,1,0:T(2,128)(2,1)S(1)}, bf16[4,4,128,2,128]{4,3,2,1,0:T(2,128)(2,1)}, u32[]{:S(2)}) copy-start(bf16[4,4,128,2,128]{4,3,2,1,0:T(2,128)(2,1)} %param.8) | copy-start | bytes 3145732
  18.7 167.7 %all-to-all-start = ((bf16[4,4,128,4,2,128]{5,3,1,0,4,2:T(4,128)(2,1)}), bf16[4,4,128,4,2,128]{5,3,1,0,4,2:T(4,128)(2,1)}, u32[]{:S(2)}, u32[]{:S(2)}) async-start(bf16[4,4,128,4,2,128]{5,3,1,0,4,2:T(4,128)(2,1)} %copy.68), calls=%async_computation | async-start | bytes 8388608 | tf_op jit(solution)/shard_map/all_to_all | solution.py:56
  30.5 250.5 %reduce-scatter.2.cloned.1.call-start = ((), (), s32[]{:S(2)}) async-start(), calls=%async_computation.3 | async-start | bytes 4718592 | tf_op jit(solution)/shard_map/reduce_scatter | solution.py:94
  165.5 5.2 %copy-start.1 = (s32[4,128,128]{2,1,0:T(8,128)S(1)}, s32[4,128,128]{2,1,0:T(8,128)}, u32[]{:S(2)}) copy-start(s32[4,128,128]{2,1,0:T(8,128)} %param.9) | copy-start | bytes 786436
  165.6 5.1 %copy-start.6 = (s32[4]{0:T(128)S(1)}, s32[4]{0:T(128)}, u32[]{:S(2)}) copy-start(s32[4]{0:T(128)} %iota_add_fusion) | copy-start | bytes 52
  175.4 3.1 %copy-start.2 = (bf16[1,128,2,128]{3,1,0,2:T(8,128)(2,1)S(1)}, bf16[1,128,2,128]{3,1,0,2:T(8,128)(2,1)}, u32[]{:S(2)}) copy-start(bf16[1,128,2,128]{3,1,0,2:T(8,128)(2,1)} %get-tuple-element.15) | copy-start | bytes 196612
  175.4 3.1 %copy-start.3 = (bf16[1,128,2,128]{3,1,0,2:T(8,128)(2,1)S(1)}, bf16[1,128,2,128]{3,1,0,2:T(8,128)(2,1)}, u32[]{:S(2)}) copy-start(bf16[1,128,2,128]{3,1,0,2:T(8,128)(2,1)} %get-tuple-element.16) | copy-start | bytes 196612
Sparse Core Ops, SparseCore 0:
  9.1 79.7 all-gather.1
  230.7 50.2 reduce-scatter.1

commit v2 on v1

v2 whole, which is shorter than its diff:
```python
import functools
import math

import jax
import jax.numpy as jnp
import numpy as np
from jax import lax
from jax.experimental import pallas as pl
from jax.experimental.pallas import tpu as pltpu
from jax.sharding import PartitionSpec as P

STEPS_CYCLE = 256
N = 128
PTS = 4
LOCAL = 4
SLABS = 32
GROUPS = 8
ROWS = N // GROUPS
F32 = jnp.float32
BF16 = jnp.bfloat16
I32 = jnp.int32
MESH = pl.DeviceIdType.MESH


def dft_pair():
    index = np.arange(N)
    angle = (index[:, None] * index[None, :] % N).astype(np.float32) * np.float32(2.0 * math.pi / N)
    cosine = np.cos(angle) / np.float32(math.sqrt(N))
    sine = np.sin(angle) / np.float32(math.sqrt(N))
    inverse = np.block([[cosine, -sine], [sine, cosine]])
    return np.stack([inverse, inverse.T]).astype(jnp.bfloat16)


def dot(a, b):
    return jnp.dot(a, b, preferred_element_type=F32)


def iotas(rows, cols):
    return (
        lax.broadcasted_iota(I32, (rows, cols), 0),
        lax.broadcasted_iota(I32, (rows, cols), 1),
    )


def as_bf16(condition):
    return jnp.where(condition, 1.0, 0.0).astype(BF16)


def lanes(parts):
    return jnp.concatenate(parts, axis=1)


def rows_of(parts):
    return jnp.concatenate(parts, axis=0)


def body(
    coef_hbm, basis, maps_hbm, field_hbm, data_hbm, mask_hbm, table_hbm, out_ref,
    coef, maps, field, mask, table, data, mix_x, mix_y, send, recv, own_mask, all_mask, mask_full,
    sens_re, sens_im, cosine, sine, image_part, image_recv, image_all, model,
    comb_part, comb_recv, comb_all, grad,
    load_sem, data_sem, self_sem, send_sem, recv_sem, mask_send, mask_recv,
    irs_send, irs_recv, iag_send, iag_recv, crs_send, crs_recv, cag_send, cag_recv,
):
    me = lax.axis_index("space")
    mg = lax.axis_index("coil")

    barrier = pltpu.get_barrier_semaphore()

    def greet_space(k, carry):
        pl.semaphore_signal(barrier, inc=1, device_id=(lax.rem(me + k, SLABS), mg), device_id_type=MESH)
        return carry

    def greet_coil(k, carry):
        pl.semaphore_signal(barrier, inc=1, device_id=(me, lax.rem(mg + k, GROUPS)), device_id_type=MESH)
        return carry

    lax.fori_loop(1, SLABS, greet_space, 0)
    lax.fori_loop(1, GROUPS, greet_coil, 0)

    loads = [
        pltpu.make_async_copy(src, dst, load_sem.at[i])
        for i, (src, dst) in enumerate(
            [(table_hbm, table), (mask_hbm, mask), (coef_hbm, coef), (maps_hbm, maps), (field_hbm, field)]
        )
    ]

    def data_load(t, c):
        return pltpu.make_async_copy(
            data_hbm.at[c, t], data.at[t, :, pl.ds(c * N, N)], data_sem.at[t, c]
        )

    loads[0].start()
    loads[1].start()
    for c in range(LOCAL):
        data_load(0, c).start()
    for load in loads[2:]:
        load.start()
    for t in range(1, PTS):
        for c in range(LOCAL):
            data_load(t, c).start()
    loads[0].wait()

    row, col = iotas(2 * N, 8 * N)
    spread = as_bf16((row % N == col // 8) & (row // N == col % 2))
    wide = dot(table[0], spread).astype(BF16)
    row, col = iotas(2 * N, N // 2)
    repeat = as_bf16(col == row // 4)
    row, col = iotas(2 * N, 8 * N)
    same_line = row % 4 == (col // 2) % 4
    for block in range(4):
        part = dot(repeat, wide[block * (N // 2) : (block + 1) * (N // 2)])
        mix_x[pl.ds(block * 2 * N, 2 * N), :] = jnp.where(same_line, part, 0.0).astype(BF16)
    loads[1].wait()
    for t in range(PTS):
        own_mask[pl.ds(t * 4, 4), :] = mask[t].astype(F32).astype(BF16)

    def data_chunk(t):
        for c in range(LOCAL):
            data_load(t, c).wait()
        lines = mask[t].astype(F32)
        lines = rows_of([lines, lines])
        lines = lanes([lines] * LOCAL)
        for half in range(2):
            parts = []
            for p in range(2):
                mixed = dot(mix_x[pl.ds((2 * p + half) * 2 * N, 2 * N), :], data[t])
                mixed = mixed.reshape(32, 8, LOCAL * N) * lines[None]
                parts.append(mixed.reshape(2 * N, LOCAL * N).astype(BF16))
            stacked = rows_of(
                [lanes([parts[0][:, c * N : (c + 1) * N], parts[1][:, c * N : (c + 1) * N]]) for c in range(LOCAL)]
            )
            turned = dot(stacked, table[1]).astype(BF16)
            for c in range(LOCAL):
                piece = turned[c * 2 * N : (c + 1) * 2 * N]
                for p in range(2):
                    send[t, pl.ds(half * 16, 16), :, pl.ds((p * LOCAL + c) * N, N)] = piece[
                        :, p * N : (p + 1) * N
                    ].reshape(16, 16, N)

    def self_copy(t):
        return pltpu.make_async_copy(send.at[t, me], recv.at[t, me], self_sem.at[t])

    def push_data(t):
        self_copy(t).start()

        def push(k, carry):
            to = lax.rem(me + k, SLABS)
            pltpu.make_async_remote_copy(
                src_ref=send.at[t, to], dst_ref=recv.at[t, me],
                send_sem=send_sem.at[t], recv_sem=recv_sem.at[t],
                device_id=(to, mg), device_id_type=MESH,
            ).start()
            return carry

        lax.fori_loop(1, SLABS, push, 0)

    def push_coil(t, part, landing, ssem, rsem):
        def push(k, carry):
            to = lax.rem(mg + k, GROUPS)
            pltpu.make_async_remote_copy(
                src_ref=part.at[t, to], dst_ref=landing.at[t, mg],
                send_sem=ssem.at[t], recv_sem=rsem.at[t],
                device_id=(me, to), device_id_type=MESH,
            ).start()
            return carry

        lax.fori_loop(1, GROUPS, push, 0)

    def push_sum(t, total, ssem, rsem):
        def push(k, carry):
            to = lax.rem(mg + k, GROUPS)
            pltpu.make_async_remote_copy(
                src_ref=total.at[t, mg], dst_ref=total.at[t, mg],
                send_sem=ssem.at[t], recv_sem=rsem.at[t],
                device_id=(me, to), device_id_type=MESH,
            ).start()
            return carry

        lax.fori_loop(1, GROUPS, push, 0)

    def drain(buffer, t, count, sem):
        view = buffer.at[t, pl.ds(0, count)]
        pltpu.make_async_copy(view, view, sem.at[t]).wait()

    def finish_sum(t, part, landing, total, rsem, ssem2, rsem2):
        drain(landing, t, GROUPS - 1, rsem)
        landing[t, mg] = part[t, mg]
        value = landing[t, 0].astype(F32)
        for j in range(1, GROUPS):
            value = value + landing[t, j].astype(F32)
        total[t, mg] = value.astype(BF16)
        push_sum(t, total, ssem2, rsem2)

    data_chunk(0)
    pl.semaphore_wait(barrier, SLABS - 1 + GROUPS - 1)
    push_data(0)

    def push_mask(k, carry):
        to = lax.rem(me + k, SLABS)
        pltpu.make_async_remote_copy(
            src_ref=own_mask, dst_ref=all_mask.at[me],
            send_sem=mask_send, recv_sem=mask_recv,
            device_id=(to, mg), device_id_type=MESH,
        ).start()
        return carry

    lax.fori_loop(1, SLABS, push_mask, 0)

    loads[2].wait()
    row, col = iotas(2 * N, 2 * N)
    untie = as_bf16(col == 2 * (row % N) + row // N)
    for x in range(LOCAL):
        pair = dot(untie, lanes([coef[0, x], coef[1, x]]))
        for t in range(PTS):
            re = im = None
            for l in range(2):
                where = (2 * mg + l) * PTS + t
                b_re, b_im = basis[where], basis[16 * PTS + where]
                x_re = pair[:N, l * N : (l + 1) * N]
                x_im = pair[N:, l * N : (l + 1) * N]
                r, i = b_re * x_re - b_im * x_im, b_re * x_im + b_im * x_re
                re, im = (r, i) if re is None else (re + r, im + i)
            image_part[t, :, 0, x] = re.astype(BF16).reshape(GROUPS, ROWS, N)
            image_part[t, :, 1, x] = im.astype(BF16).reshape(GROUPS, ROWS, N)
    for t in range(PTS):
        push_coil(t, image_part, image_recv, irs_send, irs_recv)

    def later_chunk(t, carry):
        data_chunk(t)
        push_data(t)
        return carry

    lax.fori_loop(1, PTS, later_chunk, 0)

    loads[3].wait()
    for x in range(LOCAL):
        both = dot(untie, lanes([maps[c, x] for c in range(LOCAL)]))
        sens_re[x] = both[:N]
        sens_im[x] = both[N:]
    for t in range(PTS):
        finish_sum(t, image_part, image_recv, image_all, irs_recv, iag_send, iag_recv)
    loads[4].wait()
    for x in range(LOCAL):
        angle = (field[x] & (STEPS_CYCLE - 1)).astype(F32) * (2.0 * math.pi / STEPS_CYCLE)
        c1, s1 = jnp.cos(angle), jnp.sin(angle)
        c2, s2 = c1 * c1 - s1 * s1, 2.0 * (c1 * s1)
        c3, s3 = c2 * c1 - s2 * s1, s2 * c1 + c2 * s1
        c4, s4 = c2 * c2 - s2 * s2, 2.0 * (c2 * s2)
        for t, (c, s) in enumerate([(c1, s1), (c2, s2), (c3, s3), (c4, s4)]):
            cosine[t, x] = c
            sine[t, x] = s
    row, col = iotas(2 * N, 8 * N)
    spread = as_bf16(
        (row // N == col // (4 * N)) & (row % N == 4 * ((col % (4 * N)) // 16) + col % 4)
    )
    wide = dot(table[0], spread)
    for x in range(LOCAL):
        mix_y[x] = jnp.where((col // 4) % 4 == x, wide, 0.0).astype(BF16)

    mask_view = all_mask.at[pl.ds(0, SLABS - 1)]
    pltpu.make_async_copy(mask_view, mask_view, mask_recv).wait()
    all_mask[me] = own_mask[...]
    row, col = iotas(N, SLABS * 16)
    everything = all_mask[...].reshape(SLABS * 16, N)
    for t in range(PTS):
        pick = as_bf16((col // 16 == row // 4) & (col % 4 == row % 4) & ((col // 4) % 4 == t))
        mask_full[t] = dot(pick, everything)

    def model_term(t):
        drain(image_all, t, GROUPS - 1, iag_recv)

        def one(x, carry):
            i_re = image_all[t, :, 0, x].reshape(N, N).astype(F32)
            i_im = image_all[t, :, 1, x].reshape(N, N).astype(F32)
            c, s = cosine[t, x], sine[t, x]
            t_re, t_im = c * i_re - s * i_im, s * i_re + c * i_im
            s_re, s_im = sens_re[x], sens_im[x]
            stack = []
            for k in range(LOCAL):
                a, b = s_re[:, k * N : (k + 1) * N], s_im[:, k * N : (k + 1) * N]
                stack.append(lanes([(a * t_re - b * t_im).astype(BF16), (a * t_im + b * t_re).astype(BF16)]))
            depth = dot(rows_of(stack), table[0]).astype(BF16)
            planes = rows_of(
                [lanes([depth[k * N : (k + 1) * N, p * N : (p + 1) * N] for k in range(LOCAL)]) for p in range(2)]
            )
            lines = dot(table[1], planes)
            m = lanes([mask_full[t]] * LOCAL)
            lines = rows_of([(lines[:N] * m).astype(BF16), (lines[N:] * m).astype(BF16)])
            back = dot(table[0], lines).astype(BF16)
            stack = rows_of(
                [lanes([back[p * N : (p + 1) * N, k * N : (k + 1) * N] for p in range(2)]) for k in range(LOCAL)]
            )
            back = dot(stack, table[1])
            q_re = q_im = None
            for k in range(LOCAL):
                a, b = s_re[:, k * N : (k + 1) * N], s_im[:, k * N : (k + 1) * N]
                r, i = back[k * N : (k + 1) * N, :N], back[k * N : (k + 1) * N, N:]
                u, v = a * r + b * i, a * i - b * r
                q_re, q_im = (u, v) if q_re is None else (q_re + u, q_im + v)
            model[t, x, 0] = q_re
            model[t, x, 1] = q_im
            return carry

        lax.fori_loop(0, LOCAL, one, 0)

    def model_step(t, carry):
        model_term(t)
        return carry

    lax.fori_loop(0, PTS, model_step, 0)

    def data_term(t):
        drain(recv, t, SLABS - 1, recv_sem)
        self_copy(t).wait()

        def one(x, carry):
            arrived = recv[t].reshape(SLABS * 16, 2 * LOCAL * N)
            mix = mix_y[x]
            plane = dot(mix[:, : 4 * N], arrived[:, : 4 * N]) + dot(mix[:, 4 * N :], arrived[:, 4 * N :])
            s_re, s_im = sens_re[x], sens_im[x]
            r, i = plane[:N], plane[N:]
            u, v = s_re * r + s_im * i, s_re * i - s_im * r
            q_re, q_im = model[t, x, 0], model[t, x, 1]
            for k in range(LOCAL):
                q_re = q_re - u[:, k * N : (k + 1) * N]
                q_im = q_im - v[:, k * N : (k + 1) * N]
            comb_part[t, :, 0, x] = q_re.astype(BF16).reshape(GROUPS, ROWS, N)
            comb_part[t, :, 1, x] = q_im.astype(BF16).reshape(GROUPS, ROWS, N)
            return carry

        lax.fori_loop(0, LOCAL, one, 0)
        push_coil(t, comb_part, comb_recv, crs_send, crs_recv)

    def accumulate(t):
        drain(comb_all, t, GROUPS - 1, cag_recv)
        for x in range(LOCAL):
            q_re = comb_all[t, :, 0, x].reshape(N, N).astype(F32)
            q_im = comb_all[t, :, 1, x].reshape(N, N).astype(F32)
            c, s = cosine[t, x], sine[t, x]
            w_re, w_im = c * q_re + s * q_im, c * q_im - s * q_re
            for l in range(2):
                where = (2 * mg + l) * PTS + t
                b_re, b_im = basis[where], basis[16 * PTS + where]
                g_re, g_im = b_re * w_re + b_im * w_im, b_re * w_im - b_im * w_re
                if t:
                    g_re = g_re + grad[l, x, 0]
                    g_im = g_im + grad[l, x, 1]
                if t < PTS - 1:
                    grad[l, x, 0] = g_re
                    grad[l, x, 1] = g_im
                else:
                    out_ref[l, x, pl.ds(0, N, stride=2), :] = g_re
                    out_ref[l, x, pl.ds(1, N, stride=2), :] = g_im

    finish = functools.partial(
        finish_sum, part=comb_part, landing=comb_recv, total=comb_all, rsem=crs_recv, ssem2=cag_send, rsem2=cag_recv
    )
    for t in range(PTS):
        data_term(t)
        if t >= 1:
            finish(t - 1)
        if t >= 2:
            accumulate(t - 2)
    finish(PTS - 1)
    accumulate(PTS - 2)
    accumulate(PTS - 1)

    def spent(k, carry):
        drain(send, k, SLABS - 1, send_sem)
        drain(image_part, k, GROUPS - 1, irs_send)
        drain(image_part, k, GROUPS - 1, iag_send)
        drain(comb_part, k, GROUPS - 1, crs_send)
        drain(comb_part, k, GROUPS - 1, cag_send)
        return carry

    lax.fori_loop(0, PTS, spent, 0)
    pltpu.make_async_copy(mask_view, mask_view, mask_send).wait()


def step(coef, basis, maps, field, data, mask):
    any_space = pl.BlockSpec(memory_space=pl.ANY)
    shared = (PTS, GROUPS, 2, LOCAL, ROWS, N)
    dma = pltpu.SemaphoreType.DMA
    scratch = [
        pltpu.VMEM((2, LOCAL, 2 * N, N), BF16),
        pltpu.VMEM((LOCAL, LOCAL, 2 * N, N), BF16),
        pltpu.VMEM((LOCAL, N, N), I32),
        pltpu.VMEM((PTS, 4, N), I32),
        pltpu.VMEM((2, 2 * N, 2 * N), BF16),
        pltpu.VMEM((PTS, 8 * N, LOCAL * N), BF16),
        pltpu.VMEM((8 * N, 8 * N), BF16),
        pltpu.VMEM((LOCAL, 2 * N, 8 * N), BF16),
        pltpu.VMEM((PTS, SLABS, 16, 2 * LOCAL * N), BF16),
        pltpu.VMEM((PTS, SLABS, 16, 2 * LOCAL * N), BF16),
        pltpu.VMEM((16, N), BF16),
        pltpu.VMEM((SLABS, 16, N), BF16),
        pltpu.VMEM((PTS, N, N), F32),
        pltpu.VMEM((LOCAL, N, LOCAL * N), F32),
        pltpu.VMEM((LOCAL, N, LOCAL * N), F32),
        pltpu.VMEM((PTS, LOCAL, N, N), F32),
        pltpu.VMEM((PTS, LOCAL, N, N), F32),
        pltpu.VMEM(shared, BF16),
        pltpu.VMEM(shared, BF16),
        pltpu.VMEM(shared, BF16),
        pltpu.VMEM((PTS, LOCAL, 2, N, N), F32),
        pltpu.VMEM(shared, BF16),
        pltpu.VMEM(shared, BF16),
        pltpu.VMEM(shared, BF16),
        pltpu.VMEM((2, LOCAL, 2, N, N), F32),
        dma((5,)), dma((PTS, LOCAL)), dma((PTS,)), dma((PTS,)), dma((PTS,)), dma, dma,
        dma((PTS,)), dma((PTS,)), dma((PTS,)), dma((PTS,)),
        dma((PTS,)), dma((PTS,)), dma((PTS,)), dma((PTS,)),
    ]
    out = pl.pallas_call(
        body,
        out_shape=jax.ShapeDtypeStruct((2, LOCAL, 2 * N, N), F32),
        in_specs=[any_space, pl.BlockSpec(memory_space=pltpu.SMEM)] + [any_space] * 5,
        out_specs=pl.BlockSpec(memory_space=pltpu.VMEM),
        scratch_shapes=scratch,
        compiler_params=pltpu.CompilerParams(
            collective_id=0, has_side_effects=True, vmem_limit_bytes=56 << 20
        ),
    )(
        coef.reshape(2, LOCAL, 2 * N, N),
        basis.astype(F32).reshape(-1),
        maps.reshape(LOCAL, LOCAL, 2 * N, N),
        field,
        data.reshape(LOCAL, PTS, 8 * N, N),
        mask,
        jnp.asarray(dft_pair()),
    )
    return out.reshape(2, LOCAL, N, 2, N)


def solution(mesh):
    in_specs = (
        P("coil", "space", None, None, None),
        P(),
        P("coil", "space", None, None, None),
        P("space", None, None),
        P("coil", None, None, "space", None, None),
        P(None, "space", None),
    )
    out_specs = P("coil", "space", None, None, None)
    return jax.shard_map(step, mesh=mesh, in_specs=in_specs, out_specs=out_specs, check_vma=False)
```

time: 292 us -> 134 us (0.46)
  blocking collectives: 132 us -> 0 us
  Pallas kernels: 0 us -> 129 us
  waiting for transfers between devices: 50.5 us -> 0 us
  matrix products: 35.8 us -> 0 us
  other arithmetic: 26 us -> 0 us
  local copies, waits for them, and re-layouts: 20.6 us -> 3.66 us
  between operations: 13.6 us -> 0.01 us
  starting transfers between devices: 11.8 us -> 0 us
    all_gather x1 -> x0, blocking collectives: 132 us -> none  [shards(): lax.all_gather(sample_mask.astype(jnp.bfloat16), 'space', axis=1, tiled=T...]
    pallas_call x0 -> x1, Pallas kernels: none -> 129 us  [step(): pl.pallas_call(body, out_shape=jax.ShapeDtypeStruct((2, LOCAL, 2 * N, N),...]
    reduce_scatter x1 -> x0, waiting for transfers between devices: 50.4 us -> none  [shards(): lax.psum_scatter(jnp.einsum('txypz,tplq->lxyqz', combined, adjoint_mix(se...]
    dot_general x5 -> x0, matrix products: 35.8 us -> none  [the longest x3 23 us: transform(): return jnp.einsum(form, volume, table, preferred_element_type=jnp.float32)]
    convert_element_type x4 -> x0, local copies, waits for them, and re-layouts: 18.4 us -> none  [the longest x1 7.58 us: shards(): measured.astype(jnp.float32)]
    all_to_all x1 -> x0, starting transfers between devices: 11.8 us -> none  [shards(): lax.all_to_all(data_first, 'space', split_axis=2, concat_axis=3, tiled=True)]
    add x2 -> x0, other arithmetic: 10.2 us -> none  [the longest x1 9.64 us: shards(): combined_real = cosine * sum_real + sine * sum_imaginary]
    sub x1 -> x0, other arithmetic: 4.63 us -> none  [shards(): turned_real = cosine * image_real - sine * image_imaginary]
  transfers between devices with their start and end apart: 3 -> 0, of which waited for: 1 -> 0; matrix products, arithmetic and copies ran while one was open for 12% -> 0% of each run, Pallas kernels for 0% -> 0%
where the time goes in v2:
time: 134 us; the launch traced here: 133 us
  Pallas kernels  129 us (96%)
  local copies, waits for them, and re-layouts  3.66 us (3%)
    pallas_call x1, Pallas kernels, step(): pl.pallas_call(body, out_shape=jax.ShapeDtypeStruct((2, LOCAL, 2 * N, N),...  129 us

profile of v2, /device:TPU:16, one launch (start us, length us, event | category | flops | bytes accessed | tf_op | source)
XLA Modules:
  0.0 133.1 jit_solution(7038826956959098397)
XLA Ops:
  0.0 0.8 copy.9
  0.8 0.6 reshape.24.basis
  1.4 129.5 %shard_map.73 = f32[2,4,256,128]{3,2,1,0:T(8,128)} custom-call(bf16[2,4,256,128]{3,2,1,0:T(8,128)(2,1)} %bitcast.7, f32[128]{0:T(128)} %reshape.24.basis, bf16[4,4,256,128]{3,2,1,0:T(8,128)(2,1)} %bitcast.6, s32[4,128,128]{2,1,0:T(8,128)} %field_hbm.1, bf16[4,4,1024,128]{3,2,1,0:T(8,128)(2,1)} %bitcast.4, s32[4,4,128]{2,1,0:T(4,128)} %mask_hbm.1, ...), custom_call_target="tpu_custom_call" | custom-call | tf_op jit(solution)/shard_map/pallas_call | solution.py:415
  130.9 2.3 %copy.11 = f32[2,4,128,2,128]{4,3,2,1,0:T(2,128)} copy(f32[2,4,128,2,128]{4,3,2,1,0:T(2,128)} %bitcast.5) | data formatting | bytes 2097152

commit v3 on v2

v3 whole, which is shorter than its diff:
```python
import math

import jax
import jax.numpy as jnp
import numpy as np
from jax import lax
from jax.experimental import pallas as pl
from jax.experimental.pallas import tpu as pltpu
from jax.sharding import PartitionSpec as P

STEPS_CYCLE = 256
N = 128
PTS = 4
LOCAL = 4
SLABS = 32
GROUPS = 8
RING = 4
QUARTER = N // RING
PIECES = 2 * PTS
F32 = jnp.float32
BF16 = jnp.bfloat16
I32 = jnp.int32
MESH = pl.DeviceIdType.MESH


def dft_pair():
    index = np.arange(N)
    angle = (index[:, None] * index[None, :] % N).astype(np.float32) * np.float32(2.0 * math.pi / N)
    cosine = np.cos(angle) / np.float32(math.sqrt(N))
    sine = np.sin(angle) / np.float32(math.sqrt(N))
    inverse = np.block([[cosine, -sine], [sine, cosine]])
    return np.stack([inverse, inverse.T]).astype(jnp.bfloat16)


def dot(a, b):
    return jnp.dot(a, b, preferred_element_type=F32)


def iotas(rows, cols):
    return (
        lax.broadcasted_iota(I32, (rows, cols), 0),
        lax.broadcasted_iota(I32, (rows, cols), 1),
    )


def as_bf16(condition):
    return jnp.where(condition, 1.0, 0.0).astype(BF16)


def lanes(parts):
    return jnp.concatenate(parts, axis=1)


def rows_of(parts):
    return jnp.concatenate(parts, axis=0)


def body(
    coef_hbm, basis_hbm, maps_hbm, field_hbm, data_hbm, mask_hbm, table_hbm, out_ref,
    coef, basis, maps, field, mask, table, data, mix_x, mix_y, send, recv, own_mask, all_mask, mask_full,
    sens_re, sens_im, cosine, sine, weight, model, grad,
    image_part, image_land, image_half, image_all, comb_part, comb_land, comb_half, comb_all,
    load_sem, data_sem, self_sem, send_sem, recv_sem, mask_send, mask_recv, image_sem, comb_sem,
):
    me = lax.axis_index("space")
    mg = lax.axis_index("coil")
    side = mg // RING
    place = lax.rem(mg, RING)

    barrier = pltpu.get_barrier_semaphore()

    def greet_space(k, carry):
        pl.semaphore_signal(barrier, inc=1, device_id=(lax.rem(me + k, SLABS), mg), device_id_type=MESH)
        return carry

    def greet_coil(k, carry):
        pl.semaphore_signal(barrier, inc=1, device_id=(me, lax.rem(mg + k, GROUPS)), device_id_type=MESH)
        return carry

    lax.fori_loop(1, SLABS, greet_space, 0)
    lax.fori_loop(1, GROUPS, greet_coil, 0)

    loads = [
        pltpu.make_async_copy(src, dst, load_sem.at[i])
        for i, (src, dst) in enumerate(
            [
                (table_hbm, table), (mask_hbm, mask), (coef_hbm, coef),
                (maps_hbm, maps), (field_hbm, field), (basis_hbm, basis),
            ]
        )
    ]

    def data_load(t, c):
        return pltpu.make_async_copy(
            data_hbm.at[c, t], data.at[t, :, pl.ds(c * N, N)], data_sem.at[t, c]
        )

    loads[0].start()
    loads[1].start()
    for c in range(LOCAL):
        data_load(0, c).start()
    for load in loads[2:]:
        load.start()
    for t in range(1, PTS):
        for c in range(LOCAL):
            data_load(t, c).start()
    loads[0].wait()

    row, col = iotas(2 * N, 8 * N)
    spread = as_bf16((row % N == col // 8) & (row // N == col % 2))
    wide = dot(table[0], spread).astype(BF16)
    row, col = iotas(2 * N, N // 2)
    repeat = as_bf16(col == row // 4)
    row, col = iotas(2 * N, 8 * N)
    same_line = row % 4 == (col // 2) % 4
    for block in range(4):
        part = dot(repeat, wide[block * (N // 2) : (block + 1) * (N // 2)])
        mix_x[pl.ds(block * 2 * N, 2 * N), :] = jnp.where(same_line, part, 0.0).astype(BF16)
    loads[1].wait()
    for t in range(PTS):
        own_mask[pl.ds(t * 4, 4), :] = mask[t].astype(F32).astype(BF16)

    def data_chunk(t):
        for c in range(LOCAL):
            data_load(t, c).wait()
        lines = mask[t].astype(F32)
        lines = rows_of([lines, lines])
        lines = lanes([lines] * LOCAL)
        for half in range(2):
            parts = []
            for p in range(2):
                mixed = dot(mix_x[pl.ds((2 * p + half) * 2 * N, 2 * N), :], data[t])
                mixed = mixed.reshape(32, 8, LOCAL * N) * lines[None]
                parts.append(mixed.reshape(2 * N, LOCAL * N).astype(BF16))
            stacked = rows_of(
                [lanes([parts[0][:, c * N : (c + 1) * N], parts[1][:, c * N : (c + 1) * N]]) for c in range(LOCAL)]
            )
            turned = dot(stacked, table[1])
            for h in range(2):
                for p in range(2):
                    for low in range(2):
                        piece = jnp.concatenate(
                            [
                                turned[c * 2 * N : (c + 1) * 2 * N, p * N : (p + 1) * N].reshape(16, 2, 8, N)[:, h]
                                for c in (low, 2 + low)
                            ],
                            axis=1,
                        )
                        send[t, pl.ds(half * 16, 16), h, :, pl.ds((2 * p + low) * N, N)] = piece.astype(BF16)

    def self_copy(t, h):
        return pltpu.make_async_copy(send.at[t, me, h], recv.at[t, me, h], self_sem.at[2 * t + h])

    def push_data(t):
        for h in range(2):
            self_copy(t, h).start()

            def push(k, carry):
                to = lax.rem(me + k, SLABS)
                pltpu.make_async_remote_copy(
                    src_ref=send.at[t, to, h], dst_ref=recv.at[t, me, h],
                    send_sem=send_sem.at[2 * t + h], recv_sem=recv_sem.at[2 * t + h],
                    device_id=(to, mg), device_id_type=MESH,
                ).start()
                return carry

            lax.fori_loop(1, SLABS, push, 0)

    def drain(view, sem):
        pltpu.make_async_copy(view, view, sem).wait()

    def to_ring(source, target, ssem, rsem):
        for k in (2, 1, 3):
            to = lax.rem(place + k, RING)
            pltpu.make_async_remote_copy(
                src_ref=source(to), dst_ref=target, send_sem=ssem, recv_sem=rsem,
                device_id=(me, side * RING + to), device_id_type=MESH,
            ).start()

    def ring_start(part, land, sem):
        to_ring(lambda to: part.at[to], land.at[place], sem.at[0], sem.at[1])

    def ring_sum(part, land, half, sem, lead):
        drain(land.at[pl.ds(0, RING - 1)], sem.at[1])

        def one(i, carry):
            land[place, i] = part[place, i]
            value = land[0, i].astype(F32)
            for j in range(1, RING):
                value = value + land[j, i].astype(F32)
            half[0, i] = value.astype(BF16)
            return carry

        lax.fori_loop(0, lead, one, 0)
        pltpu.make_async_remote_copy(
            src_ref=half.at[0], dst_ref=half.at[1], send_sem=sem.at[2], recv_sem=sem.at[3],
            device_id=(me, (1 - side) * RING + place), device_id_type=MESH,
        ).start()

    def pair_sum(half, total, sem, lead):
        drain(half.at[1], sem.at[3])

        def one(i, carry):
            total[place, i] = (half[0, i].astype(F32) + half[1, i].astype(F32)).astype(BF16)
            return carry

        lax.fori_loop(0, lead, one, 0)
        to_ring(lambda to: total.at[place], total.at[place], sem.at[4], sem.at[5])

    def ring_end(total, sem):
        drain(total.at[pl.ds(0, RING - 1)], sem.at[5])

    def ring_spent(part, half, total, sem):
        drain(part.at[pl.ds(0, RING - 1)], sem.at[0])
        drain(half.at[0], sem.at[2])
        drain(total.at[pl.ds(0, RING - 1)], sem.at[4])

    data_chunk(0)
    pl.semaphore_wait(barrier, SLABS - 1 + GROUPS - 1)
    push_data(0)

    def push_mask(k, carry):
        to = lax.rem(me + k, SLABS)
        pltpu.make_async_remote_copy(
            src_ref=own_mask, dst_ref=all_mask.at[me],
            send_sem=mask_send, recv_sem=mask_recv,
            device_id=(to, mg), device_id_type=MESH,
        ).start()
        return carry

    lax.fori_loop(1, SLABS, push_mask, 0)

    def later_chunk(t, carry):
        data_chunk(t)
        push_data(t)
        return carry

    lax.fori_loop(1, PTS, later_chunk, 0)

    loads[5].wait()
    rows = basis[...].astype(F32).reshape(2 * PTS, 4 * PTS)
    _, col = iotas(2 * PTS, 4 * PTS)
    for l in range(2):
        mine = jnp.sum(jnp.where(col == 2 * mg + l, rows, 0.0), axis=1, keepdims=True)
        weight[l] = jnp.broadcast_to(mine, (2 * PTS, N))
    loads[2].wait()
    row, col = iotas(2 * N, 2 * N)
    untie = as_bf16(col == 2 * (row % N) + row // N)
    for x in range(LOCAL):
        pair = dot(untie, lanes([coef[0, x], coef[1, x]]))
        for t in range(PTS):
            re = im = None
            for l in range(2):
                b_re, b_im = weight[l, pl.ds(t, 1)], weight[l, pl.ds(PTS + t, 1)]
                x_re = pair[:N, l * N : (l + 1) * N]
                x_im = pair[N:, l * N : (l + 1) * N]
                r, i = b_re * x_re - b_im * x_im, b_re * x_im + b_im * x_re
                re, im = (r, i) if re is None else (re + r, im + i)
            image_part[:, t, 0, x] = re.astype(BF16).reshape(RING, QUARTER, N)
            image_part[:, t, 1, x] = im.astype(BF16).reshape(RING, QUARTER, N)
    ring_start(image_part, image_land, image_sem)

    loads[3].wait()
    for x in range(LOCAL):
        both = dot(untie, lanes([maps[c, x] for c in range(LOCAL)]))
        sens_re[x] = both[:N]
        sens_im[x] = both[N:]
    ring_sum(image_part, image_land, image_half, image_sem, PTS)
    loads[4].wait()
    for x in range(LOCAL):
        angle = (field[x] & (STEPS_CYCLE - 1)).astype(F32) * (2.0 * math.pi / STEPS_CYCLE)
        c1, s1 = jnp.cos(angle), jnp.sin(angle)
        c2, s2 = c1 * c1 - s1 * s1, 2.0 * (c1 * s1)
        c3, s3 = c2 * c1 - s2 * s1, s2 * c1 + c2 * s1
        c4, s4 = c2 * c2 - s2 * s2, 2.0 * (c2 * s2)
        for t, (c, s) in enumerate([(c1, s1), (c2, s2), (c3, s3), (c4, s4)]):
            cosine[t, x] = c
            sine[t, x] = s
    pair_sum(image_half, image_all, image_sem, PTS)
    row, col = iotas(2 * N, 8 * N)
    spread = as_bf16(
        (row // N == col // (4 * N)) & (row % N == 4 * ((col % (4 * N)) // 16) + col % 4)
    )
    wide = dot(table[0], spread)
    for j in range(4):
        mix_y[j] = jnp.where((col // 4) % 4 == j, wide, 0.0).astype(BF16)

    mask_view = all_mask.at[pl.ds(0, SLABS - 1)]
    pltpu.make_async_copy(mask_view, mask_view, mask_recv).wait()
    all_mask[me] = own_mask[...]
    row, col = iotas(N, SLABS * 16)
    everything = all_mask[...].reshape(SLABS * 16, N)
    for t in range(PTS):
        pick = as_bf16((col // 16 == row // 4) & (col % 4 == row % 4) & ((col // 4) % 4 == t))
        mask_full[t] = dot(pick, everything)

    def model_term(t):
        def one(x, carry):
            i_re = image_all[:, t, 0, x].reshape(N, N).astype(F32)
            i_im = image_all[:, t, 1, x].reshape(N, N).astype(F32)
            c, s = cosine[t, x], sine[t, x]
            t_re, t_im = c * i_re - s * i_im, s * i_re + c * i_im
            s_re, s_im = sens_re[x], sens_im[x]
            stack = []
            for k in range(LOCAL):
                a, b = s_re[:, k * N : (k + 1) * N], s_im[:, k * N : (k + 1) * N]
                stack.append(lanes([(a * t_re - b * t_im).astype(BF16), (a * t_im + b * t_re).astype(BF16)]))
            depth = dot(rows_of(stack), table[0]).astype(BF16)
            planes = rows_of(
                [lanes([depth[k * N : (k + 1) * N, p * N : (p + 1) * N] for k in range(LOCAL)]) for p in range(2)]
            )
            lines = dot(table[1], planes)
            m = lanes([mask_full[t]] * LOCAL)
            lines = rows_of([(lines[:N] * m).astype(BF16), (lines[N:] * m).astype(BF16)])
            back = dot(table[0], lines).astype(BF16)
            stack = rows_of(
                [lanes([back[p * N : (p + 1) * N, k * N : (k + 1) * N] for p in range(2)]) for k in range(LOCAL)]
            )
            back = dot(stack, table[1])
            q_re = q_im = None
            for k in range(LOCAL):
                a, b = s_re[:, k * N : (k + 1) * N], s_im[:, k * N : (k + 1) * N]
                r, i = back[k * N : (k + 1) * N, :N], back[k * N : (k + 1) * N, N:]
                u, v = a * r + b * i, a * i - b * r
                q_re, q_im = (u, v) if q_re is None else (q_re + u, q_im + v)
            model[t, x, 0] = q_re
            model[t, x, 1] = q_im
            return carry

        lax.fori_loop(0, LOCAL, one, 0)

    def model_step(t, carry):
        model_term(t)
        return carry

    ring_end(image_all, image_sem)
    lax.fori_loop(0, PTS, model_step, 0)

    def data_term(n):
        t, h = n // 2, lax.rem(n, 2)
        drain(recv.at[t, pl.ds(0, SLABS - 1), h], recv_sem.at[n])
        self_copy(t, h).wait()

        def one(j, carry):
            x = 2 * h + j
            arrived = recv[t, :, h].reshape(SLABS * 16, 4 * N)
            q_re, q_im = model[t, x, 0], model[t, x, 1]
            for high in range(2):
                mix = mix_y[2 * high + j]
                plane = dot(mix[:, : 4 * N], arrived[:, : 2 * N]) + dot(mix[:, 4 * N :], arrived[:, 2 * N :])
                s_re = sens_re[x, :, pl.ds(high * 2 * N, 2 * N)]
                s_im = sens_im[x, :, pl.ds(high * 2 * N, 2 * N)]
                r, i = plane[:N], plane[N:]
                u, v = s_re * r + s_im * i, s_re * i - s_im * r
                q_re = q_re - u[:, :N] - u[:, N:]
                q_im = q_im - v[:, :N] - v[:, N:]
            comb_part[n, :, 0, j] = q_re.astype(BF16).reshape(RING, QUARTER, N)
            comb_part[n, :, 1, j] = q_im.astype(BF16).reshape(RING, QUARTER, N)
            return carry

        lax.fori_loop(0, 2, one, 0)
        ring_start(comb_part.at[n], comb_land.at[n], comb_sem.at[n])

    def middle(n):
        ring_sum(comb_part.at[n], comb_land.at[n], comb_half.at[n], comb_sem.at[n], 2)

    def last(n):
        pair_sum(comb_half.at[n], comb_all.at[n], comb_sem.at[n], 2)

    def accumulate(n, final):
        t, h = n // 2, n % 2 if final else lax.rem(n, 2)
        ring_end(comb_all.at[n], comb_sem.at[n])
        for j in range(2):
            x = 2 * h + j
            q_re = comb_all[n, :, 0, j].reshape(N, N).astype(F32)
            q_im = comb_all[n, :, 1, j].reshape(N, N).astype(F32)
            c, s = cosine[t, x], sine[t, x]
            w_re, w_im = c * q_re + s * q_im, c * q_im - s * q_re
            for l in range(2):
                b_re, b_im = weight[l, pl.ds(t, 1)], weight[l, pl.ds(PTS + t, 1)]
                g_re = grad[l, x, 0] + (b_re * w_re + b_im * w_im)
                g_im = grad[l, x, 1] + (b_re * w_im - b_im * w_re)
                if final:
                    out_ref[l, x, pl.ds(0, N, stride=2), :] = g_re
                    out_ref[l, x, pl.ds(1, N, stride=2), :] = g_im
                else:
                    grad[l, x, 0] = g_re
                    grad[l, x, 1] = g_im

    grad[...] = jnp.zeros(grad.shape, F32)

    def piece_step(n, carry):
        data_term(n)

        @pl.when(n >= 1)
        def _():
            middle(n - 1)

        @pl.when(n >= 2)
        def _():
            accumulate(n - 2, False)

        @pl.when(n >= 1)
        def _():
            last(n - 1)

        return carry

    lax.fori_loop(0, PIECES, piece_step, 0)
    middle(PIECES - 1)
    accumulate(PIECES - 2, True)
    last(PIECES - 1)
    accumulate(PIECES - 1, True)

    def spent(n, carry):
        drain(send.at[n // 2, pl.ds(0, SLABS - 1), lax.rem(n, 2)], send_sem.at[n])
        ring_spent(comb_part.at[n], comb_half.at[n], comb_all.at[n], comb_sem.at[n])
        return carry

    lax.fori_loop(0, PIECES, spent, 0)
    ring_spent(image_part, image_half, image_all, image_sem)
    pltpu.make_async_copy(mask_view, mask_view, mask_send).wait()


def step(coef, basis, maps, field, data, mask):
    any_space = pl.BlockSpec(memory_space=pl.ANY)
    dma = pltpu.SemaphoreType.DMA
    image = (PTS, 2, LOCAL, QUARTER, N)
    comb = (2, 2, QUARTER, N)
    scratch = [
        pltpu.VMEM((2, LOCAL, 2 * N, N), BF16),
        pltpu.VMEM((2, PTS, 4 * PTS), BF16),
        pltpu.VMEM((LOCAL, LOCAL, 2 * N, N), BF16),
        pltpu.VMEM((LOCAL, N, N), I32),
        pltpu.VMEM((PTS, 4, N), I32),
        pltpu.VMEM((2, 2 * N, 2 * N), BF16),
        pltpu.VMEM((PTS, 8 * N, LOCAL * N), BF16),
        pltpu.VMEM((8 * N, 8 * N), BF16),
        pltpu.VMEM((4, 2 * N, 8 * N), BF16),
        pltpu.VMEM((PTS, SLABS, 2, 16, 4 * N), BF16),
        pltpu.VMEM((PTS, SLABS, 2, 16, 4 * N), BF16),
        pltpu.VMEM((16, N), BF16),
        pltpu.VMEM((SLABS, 16, N), BF16),
        pltpu.VMEM((PTS, N, N), F32),
        pltpu.VMEM((LOCAL, N, LOCAL * N), F32),
        pltpu.VMEM((LOCAL, N, LOCAL * N), F32),
        pltpu.VMEM((PTS, LOCAL, N, N), F32),
        pltpu.VMEM((PTS, LOCAL, N, N), F32),
        pltpu.VMEM((2, 2 * PTS, N), F32),
        pltpu.VMEM((PTS, LOCAL, 2, N, N), F32),
        pltpu.VMEM((2, LOCAL, 2, N, N), F32),
        pltpu.VMEM((RING,) + image, BF16),
        pltpu.VMEM((RING,) + image, BF16),
        pltpu.VMEM((2,) + image, BF16),
        pltpu.VMEM((RING,) + image, BF16),
        pltpu.VMEM((PIECES, RING) + comb, BF16),
        pltpu.VMEM((PIECES, RING) + comb, BF16),
        pltpu.VMEM((PIECES, 2) + comb, BF16),
        pltpu.VMEM((PIECES, RING) + comb, BF16),
        dma((6,)), dma((PTS, LOCAL)), dma((PIECES,)), dma((PIECES,)), dma((PIECES,)), dma, dma,
        dma((6,)), dma((PIECES, 6)),
    ]
    out = pl.pallas_call(
        body,
        out_shape=jax.ShapeDtypeStruct((2, LOCAL, 2 * N, N), F32),
        in_specs=[any_space] * 7,
        out_specs=pl.BlockSpec(memory_space=pltpu.VMEM),
        scratch_shapes=scratch,
        compiler_params=pltpu.CompilerParams(
            collective_id=0, has_side_effects=True, vmem_limit_bytes=56 << 20
        ),
    )(
        coef.reshape(2, LOCAL, 2 * N, N),
        jnp.transpose(basis, (0, 2, 1)),
        maps.reshape(LOCAL, LOCAL, 2 * N, N),
        field,
        data.reshape(LOCAL, PTS, 8 * N, N),
        mask,
        jnp.asarray(dft_pair()),
    )
    return out.reshape(2, LOCAL, N, 2, N)


def solution(mesh):
    in_specs = (
        P("coil", "space", None, None, None),
        P(),
        P("coil", "space", None, None, None),
        P("space", None, None),
        P("coil", None, None, "space", None, None),
        P(None, "space", None),
    )
    out_specs = P("coil", "space", None, None, None)
    return jax.shard_map(step, mesh=mesh, in_specs=in_specs, out_specs=out_specs, check_vma=False)
```

time: 134 us -> 125 us (0.933)
  the two profiles are of different devices: /device:TPU:16 before, /device:TPU:32 now
where the time goes in v3:
time: 125 us
  Pallas kernels  123 us (98%)
  local copies, waits for them, and re-layouts  2.27 us (2%)
    pallas_call x1, Pallas kernels, step(): pl.pallas_call(body, out_shape=jax.ShapeDtypeStruct((2, LOCAL, 2 * N, N),...  123 us

profile of v3, /device:TPU:32, one launch (start us, length us, event | category | flops | bytes accessed | tf_op | source)
XLA Modules:
  0.0 125.0 jit_solution(17451833740646133526)
XLA Ops:
  0.0 122.7 %shard_map.73 = f32[2,4,256,128]{3,2,1,0:T(8,128)} custom-call(bf16[2,4,256,128]{3,2,1,0:T(8,128)(2,1)} %bitcast.8, bf16[2,4,16]{2,1,0:T(4,128)(2,1)} %bitcast.9, bf16[4,4,256,128]{3,2,1,0:T(8,128)(2,1)} %bitcast.7, s32[4,128,128]{2,1,0:T(8,128)} %field_hbm.1, bf16[4,4,1024,128]{3,2,1,0:T(8,128)(2,1)} %bitcast.5, s32[4,4,128]{2,1,0:T(4,128)} %mask_hbm.1, ...), custom_call_target="tpu_custom_call" | custom-call | tf_op jit(solution)/shard_map/pallas_call | solution.py:463
  122.7 2.3 %copy.9 = f32[2,4,128,2,128]{4,3,2,1,0:T(2,128)} copy(f32[2,4,128,2,128]{4,3,2,1,0:T(2,128)} %bitcast.6) | data formatting | bytes 2097152

commit v4 on v3

--- a/solution.py
+++ b/solution.py
@@ -16,6 +16,7 @@
 GROUPS = 8
 RING = 4
 QUARTER = N // RING
+ROWS = N // GROUPS
 PIECES = 2 * PTS
 F32 = jnp.float32
 BF16 = jnp.bfloat16
@@ -59,8 +60,8 @@
     coef_hbm, basis_hbm, maps_hbm, field_hbm, data_hbm, mask_hbm, table_hbm, out_ref,
     coef, basis, maps, field, mask, table, data, mix_x, mix_y, send, recv, own_mask, all_mask, mask_full,
     sens_re, sens_im, cosine, sine, weight, model, grad,
-    image_part, image_land, image_half, image_all, comb_part, comb_land, comb_half, comb_all,
-    load_sem, data_sem, self_sem, send_sem, recv_sem, mask_send, mask_recv, image_sem, comb_sem,
+    image_part, image_land, image_half, image_all, comb_part, comb_land, comb_half, comb_all, end_land,
+    load_sem, data_sem, self_sem, send_sem, recv_sem, mask_send, mask_recv, image_sem, comb_sem, end_sem,
 ):
     me = lax.axis_index("space")
     mg = lax.axis_index("coil")
@@ -151,20 +152,24 @@
     def self_copy(t, h):
         return pltpu.make_async_copy(send.at[t, me, h], recv.at[t, me, h], self_sem.at[2 * t + h])
 
-    def push_data(t):
-        for h in range(2):
-            self_copy(t, h).start()
-
-            def push(k, carry):
-                to = lax.rem(me + k, SLABS)
-                pltpu.make_async_remote_copy(
-                    src_ref=send.at[t, to, h], dst_ref=recv.at[t, me, h],
-                    send_sem=send_sem.at[2 * t + h], recv_sem=recv_sem.at[2 * t + h],
-                    device_id=(to, mg), device_id_type=MESH,
-                ).start()
-                return carry
-
-            lax.fori_loop(1, SLABS, push, 0)
+    def push_piece(n):
+        t, h = n // 2, n % 2
+        self_copy(t, h).start()
+
+        def push(k, carry):
+            to = lax.rem(me + k, SLABS)
+            pltpu.make_async_remote_copy(
+                src_ref=send.at[t, to, h], dst_ref=recv.at[t, me, h],
+                send_sem=send_sem.at[n], recv_sem=recv_sem.at[n],
+                device_id=(to, mg), device_id_type=MESH,
+            ).start()
+            return carry
+
+        lax.fori_loop(1, SLABS, push, 0)
+
+    def arrive(n):
+        drain(recv.at[n // 2, pl.ds(0, SLABS - 1), n % 2], recv_sem.at[n])
+        self_copy(n // 2, n % 2).wait()
 
     def drain(view, sem):
         pltpu.make_async_copy(view, view, sem).wait()
@@ -217,7 +222,8 @@
 
     data_chunk(0)
     pl.semaphore_wait(barrier, SLABS - 1 + GROUPS - 1)
-    push_data(0)
+    push_piece(0)
+    push_piece(1)
 
     def push_mask(k, carry):
         to = lax.rem(me + k, SLABS)
@@ -230,12 +236,15 @@
 
     lax.fori_loop(1, SLABS, push_mask, 0)
 
+    data_chunk(1)
+    push_piece(2)
+    push_piece(3)
+
     def later_chunk(t, carry):
         data_chunk(t)
-        push_data(t)
         return carry
 
-    lax.fori_loop(1, PTS, later_chunk, 0)
+    lax.fori_loop(2, PTS, later_chunk, 0)
 
     loads[5].wait()
     rows = basis[...].astype(F32).reshape(2 * PTS, 4 * PTS)
@@ -334,12 +343,15 @@
         return carry
 
     ring_end(image_all, image_sem)
-    lax.fori_loop(0, PTS, model_step, 0)
+    arrive(0)
+    push_piece(4)
+    lax.fori_loop(0, 2, model_step, 0)
+    arrive(1)
+    push_piece(5)
+    lax.fori_loop(2, PTS, model_step, 0)
 
     def data_term(n):
-        t, h = n // 2, lax.rem(n, 2)
-        drain(recv.at[t, pl.ds(0, SLABS - 1), h], recv_sem.at[n])
-        self_copy(t, h).wait()
+        t, h = n // 2, n % 2
 
         def one(j, carry):
             x = 2 * h + j
@@ -359,8 +371,6 @@
             return carry
 
         lax.fori_loop(0, 2, one, 0)
-        ring_start(comb_part.at[n], comb_land.at[n], comb_sem.at[n])
-
     def middle(n):
         ring_sum(comb_part.at[n], comb_land.at[n], comb_half.at[n], comb_sem.at[n], 2)
 
@@ -368,8 +378,9 @@
         pair_sum(comb_half.at[n], comb_all.at[n], comb_sem.at[n], 2)
 
     def accumulate(n, final):
-        t, h = n // 2, n % 2 if final else lax.rem(n, 2)
-        ring_end(comb_all.at[n], comb_sem.at[n])
+        t, h = n // 2, n % 2
+        if not (final and n == PIECES - 1):
+            ring_end(comb_all.at[n], comb_sem.at[n])
         for j in range(2):
             x = 2 * h + j
             q_re = comb_all[n, :, 0, j].reshape(N, N).astype(F32)
@@ -389,36 +400,80 @@
 
     grad[...] = jnp.zeros(grad.shape, F32)
 
-    def piece_step(n, carry):
+    def begin(n):
         data_term(n)
-
-        @pl.when(n >= 1)
-        def _():
-            middle(n - 1)
-
-        @pl.when(n >= 2)
-        def _():
-            accumulate(n - 2, False)
-
-        @pl.when(n >= 1)
-        def _():
-            last(n - 1)
-
-        return carry
-
-    lax.fori_loop(0, PIECES, piece_step, 0)
-    middle(PIECES - 1)
-    accumulate(PIECES - 2, True)
-    last(PIECES - 1)
+        ring_start(comb_part.at[n], comb_land.at[n], comb_sem.at[n])
+
+    begin(0)
+    begin(1)
+    arrive(2)
+    begin(2)
+    arrive(3)
+    begin(3)
+    push_piece(6)
+    arrive(4)
+    begin(4)
+    for n in range(4):
+        middle(n)
+    arrive(5)
+    begin(5)
+    for n in range(4):
+        last(n)
+    middle(4)
+    push_piece(7)
+    arrive(6)
+    begin(6)
+    for n in range(4):
+        accumulate(n, False)
+    last(4)
+    middle(5)
+    arrive(7)
+    data_term(PIECES - 1)
+    end_part, end_all = comb_part.at[PIECES - 1], comb_all.at[PIECES - 1]
+
+    def slot(ref, q, half):
+        return ref.at[q, :, :, pl.ds(pl.multiple_of(half * ROWS, ROWS), ROWS)]
+
+    def to_group(source, target, ssem, rsem):
+        for across, k in ((1, 2), (1, 1), (1, 3), (0, 2), (1, 0), (0, 1), (0, 3)):
+            to_side = lax.rem(side + across, 2)
+            to = lax.rem(place + k, RING)
+            pltpu.make_async_remote_copy(
+                src_ref=source(to, to_side), dst_ref=target, send_sem=ssem, recv_sem=rsem,
+                device_id=(me, to_side * RING + to), device_id_type=MESH,
+            ).start()
+
+    to_group(lambda q, half: slot(end_part, q, half), end_land.at[mg], end_sem.at[0], end_sem.at[1])
+    middle(6)
+    last(5)
+    drain(end_land.at[pl.ds(0, GROUPS - 1)], end_sem.at[1])
+    end_land[mg] = slot(end_part, place, side)[...]
+    value = end_land[0].astype(F32)
+    for j in range(1, GROUPS):
+        value = value + end_land[j].astype(F32)
+    slot(end_all, place, side)[...] = value.astype(BF16)
+    mine = slot(end_all, place, side)
+    to_group(lambda q, half: mine, mine, end_sem.at[2], end_sem.at[3])
+    last(6)
+    accumulate(4, False)
+    accumulate(5, False)
+    accumulate(6, True)
+    drain(end_land.at[pl.ds(0, GROUPS - 1)], end_sem.at[3])
     accumulate(PIECES - 1, True)
 
     def spent(n, carry):
         drain(send.at[n // 2, pl.ds(0, SLABS - 1), lax.rem(n, 2)], send_sem.at[n])
-        ring_spent(comb_part.at[n], comb_half.at[n], comb_all.at[n], comb_sem.at[n])
+
+        @pl.when(n < PIECES - 1)
+        def _():
+            ring_spent(comb_part.at[n], comb_half.at[n], comb_all.at[n], comb_sem.at[n])
+
         return carry
 
     lax.fori_loop(0, PIECES, spent, 0)
     ring_spent(image_part, image_half, image_all, image_sem)
+    drain(end_land.at[pl.ds(0, GROUPS - 1)], end_sem.at[0])
+    drain(end_land.at[pl.ds(0, GROUPS - 1)], end_sem.at[2])
     pltpu.make_async_copy(mask_view, mask_view, mask_send).wait()
 
 
@@ -457,8 +512,9 @@
         pltpu.VMEM((PIECES, RING) + comb, BF16),
         pltpu.VMEM((PIECES, 2) + comb, BF16),
         pltpu.VMEM((PIECES, RING) + comb, BF16),
+        pltpu.VMEM((GROUPS, 2, 2, ROWS, N), BF16),
         dma((6,)), dma((PTS, LOCAL)), dma((PIECES,)), dma((PIECES,)), dma((PIECES,)), dma, dma,
-        dma((6,)), dma((PIECES, 6)),
+        dma((6,)), dma((PIECES, 6)), dma((4,)),
     ]
     out = pl.pallas_call(
         body,
@@ -467,16 +523,21 @@
         out_specs=pl.BlockSpec(memory_space=pltpu.VMEM),
         scratch_shapes=scratch,
         compiler_params=pltpu.CompilerParams(
-            collective_id=0, has_side_effects=True, vmem_limit_bytes=56 << 20
+            collective_id=0, has_side_effects=True, vmem_limit_bytes=44 << 20
         ),
     )(
-        coef.reshape(2, LOCAL, 2 * N, N),
-        jnp.transpose(basis, (0, 2, 1)),
-        maps.reshape(LOCAL, LOCAL, 2 * N, N),
-        field,
-        data.reshape(LOCAL, PTS, 8 * N, N),
-        mask,
-        jnp.asarray(dft_pair()),
+        *[
+            pltpu.with_memory_space_constraint(value, pltpu.HBM)
+            for value in (
+                coef.reshape(2, LOCAL, 2 * N, N),
+                jnp.transpose(basis, (0, 2, 1)),
+                maps.reshape(LOCAL, LOCAL, 2 * N, N),
+                field,
+                data.reshape(LOCAL, PTS, 8 * N, N),
+                mask,
+                jnp.asarray(dft_pair()),
+            )
+        ]
     )
     return out.reshape(2, LOCAL, N, 2, N)
 

time: 125 us -> 118 us (0.944)
  the two profiles are of different devices: /device:TPU:32 before, /device:TPU:16 now
where the time goes in v4:
time: 118 us
  Pallas kernels  117 us (99%)
    pallas_call x1, Pallas kernels, step(): pl.pallas_call(body, out_shape=jax.ShapeDtypeStruct((2, LOCAL, 2 * N, N),...  117 us

profile of v4, /device:TPU:16, one launch (start us, length us, event | category | flops | bytes accessed | tf_op | source)
XLA Modules:
  0.0 118.2 jit_solution(11671269375494298331)
XLA Ops:
  0.0 117.2 %shard_map.73 = f32[2,4,256,128]{3,2,1,0:T(8,128)S(1)} custom-call(bf16[2,4,256,128]{3,2,1,0:T(8,128)(2,1)} %bitcast.8, bf16[2,4,16]{2,1,0:T(4,128)(2,1)} %bitcast.9, bf16[4,4,256,128]{3,2,1,0:T(8,128)(2,1)} %bitcast.7, s32[4,128,128]{2,1,0:T(8,128)} %field_hbm.1, bf16[4,4,1024,128]{3,2,1,0:T(8,128)(2,1)} %bitcast.6, s32[4,4,128]{2,1,0:T(4,128)} %mask_hbm.1, ...), custom_call_target="tpu_custom_call" | custom-call | tf_op jit(solution)/shard_map/pallas_call | solution.py:519
  117.2 1.0 copy.9

commit v5 on v4

--- a/solution.py
+++ b/solution.py
@@ -236,16 +236,6 @@
 
     lax.fori_loop(1, SLABS, push_mask, 0)
 
-    data_chunk(1)
-    push_piece(2)
-    push_piece(3)
-
-    def later_chunk(t, carry):
-        data_chunk(t)
-        return carry
-
-    lax.fori_loop(2, PTS, later_chunk, 0)
-
     loads[5].wait()
     rows = basis[...].astype(F32).reshape(2 * PTS, 4 * PTS)
     _, col = iotas(2 * PTS, 4 * PTS)
@@ -269,12 +259,22 @@
             image_part[:, t, 1, x] = im.astype(BF16).reshape(RING, QUARTER, N)
     ring_start(image_part, image_land, image_sem)
 
+    data_chunk(1)
+    push_piece(2)
+
+    def later_chunk(t, carry):
+        data_chunk(t)
+        return carry
+
+    lax.fori_loop(2, PTS, later_chunk, 0)
+
     loads[3].wait()
     for x in range(LOCAL):
         both = dot(untie, lanes([maps[c, x] for c in range(LOCAL)]))
         sens_re[x] = both[:N]
         sens_im[x] = both[N:]
     ring_sum(image_part, image_land, image_half, image_sem, PTS)
+    push_piece(3)
     loads[4].wait()
     for x in range(LOCAL):
         angle = (field[x] & (STEPS_CYCLE - 1)).astype(F32) * (2.0 * math.pi / STEPS_CYCLE)
@@ -286,6 +286,8 @@
             cosine[t, x] = c
             sine[t, x] = s
     pair_sum(image_half, image_all, image_sem, PTS)
+    arrive(0)
+    push_piece(4)
     row, col = iotas(2 * N, 8 * N)
     spread = as_bf16(
         (row // N == col // (4 * N)) & (row % N == 4 * ((col % (4 * N)) // 16) + col % 4)
@@ -343,12 +345,9 @@
         return carry
 
     ring_end(image_all, image_sem)
-    arrive(0)
-    push_piece(4)
-    lax.fori_loop(0, 2, model_step, 0)
     arrive(1)
     push_piece(5)
-    lax.fori_loop(2, PTS, model_step, 0)
+    lax.fori_loop(0, PTS, model_step, 0)
 
     def data_term(n):
         t, h = n // 2, n % 2

time: 118 us -> 118 us (level)
  no operation moved by 1% of the time
where the time goes in v5:
time: 118 us; the launch traced here: 117 us
  Pallas kernels  116 us (98%)
    pallas_call x1, Pallas kernels, step(): pl.pallas_call(body, out_shape=jax.ShapeDtypeStruct((2, LOCAL, 2 * N, N),...  116 us

profile of v5, /device:TPU:16, one launch (start us, length us, event | category | flops | bytes accessed | tf_op | source)
XLA Modules:
  0.0 117.5 jit_solution(15921354380141750929)
XLA Ops:
  0.0 116.5 %shard_map.73 = f32[2,4,256,128]{3,2,1,0:T(8,128)S(1)} custom-call(bf16[2,4,256,128]{3,2,1,0:T(8,128)(2,1)} %bitcast.8, bf16[2,4,16]{2,1,0:T(4,128)(2,1)} %bitcast.9, bf16[4,4,256,128]{3,2,1,0:T(8,128)(2,1)} %bitcast.7, s32[4,128,128]{2,1,0:T(8,128)} %field_hbm.1, bf16[4,4,1024,128]{3,2,1,0:T(8,128)(2,1)} %bitcast.6, s32[4,4,128]{2,1,0:T(4,128)} %mask_hbm.1, ...), custom_call_target="tpu_custom_call" | custom-call | tf_op jit(solution)/shard_map/pallas_call | solution.py:518
  116.5 1.0 copy.9

commit v6 on v5

--- a/solution.py
+++ b/solution.py
@@ -403,13 +403,13 @@
         data_term(n)
         ring_start(comb_part.at[n], comb_land.at[n], comb_sem.at[n])
 
+    arrive(2)
+    push_piece(6)
     begin(0)
     begin(1)
-    arrive(2)
     begin(2)
     arrive(3)
     begin(3)
-    push_piece(6)
     arrive(4)
     begin(4)
     for n in range(4):

time: 118 us -> 118 us (level)
  no operation moved by 1% of the time
where the time goes in v6:
time: 118 us; the launch traced here: 117 us
  Pallas kernels  116 us (98%)
    pallas_call x1, Pallas kernels, step(): pl.pallas_call(body, out_shape=jax.ShapeDtypeStruct((2, LOCAL, 2 * N, N),...  116 us

profile of v6, /device:TPU:16, one launch (start us, length us, event | category | flops | bytes accessed | tf_op | source)
XLA Modules:
  0.0 117.5 jit_solution(708128228241763014)
XLA Ops:
  0.0 116.5 %shard_map.73 = f32[2,4,256,128]{3,2,1,0:T(8,128)S(1)} custom-call(bf16[2,4,256,128]{3,2,1,0:T(8,128)(2,1)} %bitcast.8, bf16[2,4,16]{2,1,0:T(4,128)(2,1)} %bitcast.9, bf16[4,4,256,128]{3,2,1,0:T(8,128)(2,1)} %bitcast.7, s32[4,128,128]{2,1,0:T(8,128)} %field_hbm.1, bf16[4,4,1024,128]{3,2,1,0:T(8,128)(2,1)} %bitcast.6, s32[4,4,128]{2,1,0:T(4,128)} %mask_hbm.1, ...), custom_call_target="tpu_custom_call" | custom-call | tf_op jit(solution)/shard_map/pallas_call | solution.py:518
  116.5 1.0 copy.9
